TPU v7x, 256 devices: a whole 4x4x8 slice. The times are simulated.
256 devices in a mesh: illum: 32 (over z_hi, x, y), row: 8 (over z_lo, core).
Axes of the slice: x: 4, y: 4, z: 8 (z_hi: 2, z_lo: 4; z = z_hi * 4 + z_lo), core: 2. Of those that a mesh axis runs over, the one named last changes fastest.
Arguments:
- angles: int32 [128, 2], P('illum'), may hold values from -8 to 8
- depth_order: int32 [3], replicated, may hold values from 0 to 31, as said below
- slices: float32 [32, 64, 4096], P('illum', 'row'), may hold values from -4 to 4
- cotangent: float32 [128, 2, 64, 4096], P('illum', None, 'row'), may hold values from -0.6 to 0.6
Outputs:
- exit_field: float32 [128, 2, 64, 4096], P('illum', None, 'row')
- slice_grad: float32 [32, 64, 4096], P('illum', 'row')
Inputs may be any that keep to these rules, and one draw needn't show every extreme that they name: `depth_order`: 3 distinct slice numbers; slice 0 and the last slice are always among them.
All inputs are finite; a program needn't handle non-finite values.
Results may differ from a plain program's by a relative error of at most 0.0001.
Values sent between devices are 32-bit elements; how exact they have to be, the bound alone decides.
No kernel may reach another device: no remote copies, remote signals or barrier semaphores. Data moves between devices by JAX's collectives and lax.ppermute only.
A program may use at most 64 MiB of HBM per device.

v0:
```python
import functools
import math

import jax
import jax.numpy as jnp
from jax import lax
from jax.experimental import pallas as pl
from jax.experimental.pallas import tpu as pltpu
from jax.sharding import PartitionSpec as P


rate_scale = 0.3
ROWS = 8
COLS = 4096
TILES = COLS // 128
LAYERS = 3
HALO = 8
EXT = ROWS + 2 * HALO
N_ROW = 8
NX = ROWS * N_ROW
PAD = 144
PLANE = 16

SIN_C = (0.9999999996397458, -0.16666666036106006, 0.00833331543673961,
         -0.00019839409893936808, 2.7469726872825416e-06, -2.3138942785856126e-08)
COS_C = (0.9999999953627682, -0.49999991881071015, 0.04166643614419552,
         -0.001388649171259302, 2.4688583708756773e-05, -2.5084304017242627e-07)


def horner(coefs, z):
    r = z * coefs[-1] + coefs[-2]
    for c in coefs[-3::-1]:
        r = r * z + c
    return r


def sincos(x):
    y = x * 0.5
    z = y * y
    s = y * horner(SIN_C, z)
    c = horner(COS_C, z)
    s2 = s + s
    return s2 * c, 1.0 - s2 * s


def chunk(j):
    return slice(8 * j, 8 * j + 8)


def padded(j, shift=0):
    return slice(8 + 8 * j + shift, 16 + 8 * j + shift)


def fill_pads(ref, rows):
    flat = ref.reshape(rows * 2 * PAD, 128)
    tile = lax.broadcasted_iota(jnp.int32, (rows * 2, 128), 1) & (TILES - 1)
    high = flat[pl.ds(135, rows * 2, stride=PAD), :]
    low = flat[pl.ds(8, rows * 2, stride=PAD), :]
    flat[pl.ds(7, rows * 2, stride=PAD), :] = jnp.where(tile == 0, 0.0, pltpu.roll(high, 1, 1))
    flat[pl.ds(136, rows * 2, stride=PAD), :] = jnp.where(
        tile == TILES - 1, 0.0, pltpu.roll(low, 127, 1))


def clear_outside(row, ref, base, rows):
    for at in (base - 1 - ROWS * row, base + NX - ROWS * row):
        @pl.when((at >= 0) & (at < rows))
        def _(at=at):
            ref[at] = jnp.zeros((2, PAD, 128), jnp.float32)


def lap_pair(src, r, k, j):
    v = [src[r + q, k, padded(j), :] for q in (-1, 0, 1, 2)]
    out = []
    for q in (0, 1):
        side = src[r + q, k, padded(j, -1), :] + src[r + q, k, padded(j, 1), :]
        out.append((v[q] + v[q + 2]) + side - 4.0 * v[q + 1])
    return out


def step(row, src, rows, base, h, powers, factor, write):
    prev = src
    for n, dst in enumerate(powers):
        lo, count = base - h + 1 + n, ROWS + 2 * (h - 1 - n)

        def body(i, _, prev=prev, dst=dst, lo=lo):
            r = lo + 2 * i
            for k in range(2):
                for j in range(16):
                    pair = lap_pair(prev, r, k, j)
                    for q in (0, 1):
                        dst[r + q, k, padded(j), :] = pair[q]
            return 0

        lax.fori_loop(0, count // 2, body, 0)
        fill_pads(dst, rows)
        clear_outside(row, dst, base, rows)
        prev = dst
    l1, l2, l3 = powers
    c1, c2, c3, c4 = factor, -factor**2 / 2, -factor**3 / 6, factor**4 / 24
    lo = base - h + 4

    def last(i, _):
        r = lo + 2 * i
        for j in range(16):
            l4 = [lap_pair(l3, r, k, j) for k in range(2)]
            for q in (0, 1):
                even, odd = [], []
                for k in range(2):
                    at = (r + q, k, padded(j), slice(None))
                    even.append(src[at] + (c2 * l2[at] + c4 * l4[k][q]))
                    odd.append(c1 * l1[at] + c3 * l3[at])
                write(r + q, j, even[0] - odd[1], even[1] + odd[0])
        return 0

    lax.fori_loop(0, (ROWS + 2 * (h - 4)) // 2, last, 0)


def natural(g, k, r):
    return pl.ds((g * 2 + k) * TILES * ROWS + r, TILES, stride=ROWS)


def turned(cot, k, r):
    return jnp.concatenate([cot[natural(g, k, r), :] for g in range(4)], axis=0).T


def split_kernel(ids, cot, out, send_e, send_o, own, sem):
    def body(r, _):
        for k in range(2):
            own[r, k] = turned(cot, k, r)
        return 0

    lax.fori_loop(0, ROWS, body, 0)
    keep = pltpu.make_async_copy(own, out, sem)
    keep.start()
    odd = ids[0] & 1
    for r in range(4):
        send_e[r] = own[r + 4 * (1 - odd)]
        send_o[r] = own[r + 4 * odd]
    keep.wait()


def put(dst, at, src, n):
    def body(r, _):
        for k in range(2):
            dst[at + r, k, 8:136, :] = src[r, k]
        return 0

    lax.fori_loop(0, n, body, 0)


def adjoint_kernel(ids, own, got_e, got_o, out, own_v, res, u, l1, l2, l3, sem):
    row = ids[0]
    odd = row & 1
    fetch = pltpu.make_async_copy(own, own_v, sem)
    fetch.start()
    put(u, 12 - 12 * odd, got_e, 4)
    put(u, 12 * odd, got_o, 4)
    fetch.wait()
    put(u, 4, own_v, 8)
    fill_pads(u, 16)

    def write(r, j, re, im):
        res[r - 4, 0, chunk(j), :] = re
        res[r - 4, 1, chunk(j), :] = im

    step(row, u, 16, 4, 4, (l1, l2, l3), -rate_scale, write)
    give = pltpu.make_async_copy(res, out, sem)
    give.start()
    give.wait()


def exit_kernel(ids, sent_e, sent_o, got_e, got_o, out, u, l1, l2, l3, res):
    row = ids[0]
    odd = row & 1
    put(u, 8 - 4 * odd, sent_e, 4)
    put(u, 4 + 4 * odd, sent_o, 4)
    put(u, 12 - 12 * odd, got_e, 4)
    put(u, 12 * odd, got_o, 4)
    fill_pads(u, 16)

    def write(r, j, re, im):
        res[r - 4, 0, chunk(j), :] = re
        res[r - 4, 1, chunk(j), :] = im

    step(row, u, 16, 4, 4, (l1, l2, l3), rate_scale, write)

    def body(r, _):
        for k in range(2):
            x = res[r, k].T
            for g in range(4):
                out[natural(g, k, r), :] = x[g * TILES:(g + 1) * TILES]
        return 0

    lax.fori_loop(0, ROWS, body, 0)


def trig_tables(phases, cos_n, sin_n):
    def body(i, _):
        at = pl.ds(pl.multiple_of(i * 48, 8), 48)
        s, c = sincos(phases[at, :])
        sin_n[at, :] = s
        cos_n[at, :] = c
        return 0

    lax.fori_loop(0, TILES // 2, body, 0)


def spread(ref, n):
    x = ref[pl.ds(n, TILES, stride=LAYERS * ROWS), :]
    return jnp.concatenate([x] * 4, axis=0).T


def phase_kernel(phases, cos_out, sin_out, cos_n, sin_n):
    trig_tables(phases, cos_n, sin_n)

    def body(i, _):
        for n in (2 * i, 2 * i + 1):
            cos_out[n] = spread(cos_n, n)
            sin_out[n] = spread(sin_n, n)
        return 0

    lax.fori_loop(0, LAYERS * ROWS // 2, body, 0)


def forward_kernel(ids, angles, ph_e, ph_o, cos_own, sin_own,
                   cosr, sinr, keep0, keep1, keep2, last_e, last_o,
                   cos_n, sin_n, beam, u, v, l1, l2, l3):
    row = ids[0]
    odd = row & 1
    for ph, above in ((ph_e, odd), (ph_o, 1 - odd)):
        trig_tables(ph, cos_n, sin_n)
        first = (HALO + ROWS) * (1 - above)
        for layer in range(LAYERS):
            lo, count = (4 * above, 4) if layer == 1 else (0, 8)

            def body(i, _, layer=layer, first=first, lo=lo):
                for q in range(2):
                    r = lo + 2 * i + q
                    cosr[layer * EXT + first + r] = spread(cos_n, layer * ROWS + r)
                    sinr[layer * EXT + first + r] = spread(sin_n, layer * ROWS + r)
                return 0

            lax.fori_loop(0, count // 2, body, 0)
    for layer in range(LAYERS):
        def copy(r, _, layer=layer):
            cosr[layer * EXT + HALO + r] = cos_own[layer * ROWS + r]
            sinr[layer * EXT + HALO + r] = sin_own[layer * ROWS + r]
            return 0

        lax.fori_loop(0, ROWS, copy, 0)

    lane = lax.broadcasted_iota(jnp.int32, (8, 128), 1)
    sub = lax.broadcasted_iota(jnp.int32, (8, 128), 0)
    beam_of = lane >> 5
    pv, qv = [
        jnp.where(beam_of < 2,
                  jnp.where(beam_of == 0, angles[0, n], angles[1, n]),
                  jnp.where(beam_of == 2, angles[2, n], angles[3, n]))
        for n in range(2)
    ]
    for j in range(16):
        col = (lane & (TILES - 1)) * 128 + sub + 8 * j
        k = (qv * col) & (COLS - 1)
        s, c = sincos((k - COLS // 2).astype(jnp.float32) * (2.0 * math.pi / COLS))
        beam[0, chunk(j), :] = -c
        beam[1, chunk(j), :] = -s

    phase_at = functools.partial(rotation, cosr, sinr)

    def incident(r, _):
        k = (pv * (row * ROWS + r - HALO)) & (NX - 1)
        sa, ca = sincos((k - NX // 2).astype(jnp.float32) * (2.0 * math.pi / NX))
        for j in range(16):
            c, s = phase_at(0, r, j)
            a = sa * s - ca * c
            b = -(sa * c + ca * s)
            er, ei = beam[0, chunk(j), :], beam[1, chunk(j), :]
            u[r, 0, padded(j), :] = er * a - ei * b
            u[r, 1, padded(j), :] = ei * a + er * b
        return 0

    lax.fori_loop(0, EXT, incident, 0)
    fill_pads(u, EXT)
    clear_outside(row, u, HALO, EXT)

    def write_v(r, j, re, im):
        c, s = phase_at(1, r, j)
        v[r, 0, padded(j), :] = re * c - im * s
        v[r, 1, padded(j), :] = re * s + im * c

    step(row, u, EXT, HALO, 8, (l1, l2, l3), rate_scale, write_v)
    fill_pads(v, EXT)
    clear_outside(row, v, HALO, EXT)

    def write_last(r, j, re, im):
        c, s = phase_at(2, r, j)
        keep2[r - HALO, 0, chunk(j), :] = re * c - im * s
        keep2[r - HALO, 1, chunk(j), :] = re * s + im * c

    step(row, v, EXT, HALO, 4, (l1, l2, l3), rate_scale, write_last)

    def keep(r, _):
        for k in range(2):
            keep0[r, k] = u[HALO + r, k, 8:136, :]
            keep1[r, k] = v[HALO + r, k, 8:136, :]
        return 0

    lax.fori_loop(0, ROWS, keep, 0)
    for r in range(4):
        last_e[r] = keep2[r + 4 * (1 - odd)]
        last_o[r] = keep2[r + 4 * odd]


def rotation(cosr, sinr, layer, r, j):
    return cosr[layer * EXT + r, chunk(j), :], sinr[layer * EXT + r, chunk(j), :]


def back_kernel(ids, cosr, sinr, keep0, keep1, keep2, w1, w_e, w_o, terms,
                w, w2, raw, l1, l2, l3):
    row = ids[0]
    odd = row & 1
    phase_at = functools.partial(rotation, cosr, sinr)

    def term(layer, adjoint, stored):
        def body(i, _):
            for r in (2 * i, 2 * i + 1):
                x = adjoint(r, 1) * stored(r, 0) - adjoint(r, 0) * stored(r, 1)
                x = x.T
                x = (x[:TILES] + x[TILES:2 * TILES]) + (x[2 * TILES:3 * TILES] + x[3 * TILES:])
                terms[pl.ds(layer * ROWS + r, TILES, stride=LAYERS * ROWS), :] = x
            return 0

        lax.fori_loop(0, ROWS // 2, body, 0)

    def of(ref, at=0):
        return lambda r, k: ref[at + r, k]

    for src, at in ((w1, HALO), (w_e, 16 - 16 * odd), (w_o, 16 * odd)):
        def back(r, _, src=src, at=at):
            for j in range(16):
                c, s = phase_at(2, at + r, j)
                re, im = src[r, 0, chunk(j), :], src[r, 1, chunk(j), :]
                w[at + r, 0, padded(j), :] = re * c + im * s
                w[at + r, 1, padded(j), :] = im * c - re * s
            return 0

        lax.fori_loop(0, ROWS, back, 0)
    term(2, of(w1), of(keep2))
    fill_pads(w, EXT)
    clear_outside(row, w, HALO, EXT)

    def mid(r, j, re, im):
        c, s = phase_at(1, r, j)
        raw[r - 4, 0, chunk(j), :] = re
        raw[r - 4, 1, chunk(j), :] = im
        w2[r, 0, padded(j), :] = re * c + im * s
        w2[r, 1, padded(j), :] = im * c - re * s

    step(row, w, EXT, HALO, 8, (l1, l2, l3), -rate_scale, mid)
    fill_pads(w2, EXT)
    clear_outside(row, w2, HALO, EXT)
    term(1, of(raw, 4), of(keep1))

    def final(r, j, re, im):
        raw[r - 4, 0, chunk(j), :] = re
        raw[r - 4, 1, chunk(j), :] = im

    step(row, w2, EXT, HALO, 4, (l1, l2, l3), -rate_scale, final)
    term(0, of(raw, 4), of(keep0))


def pick_kernel(ids, got, out):
    for layer in range(LAYERS):
        for t in range(2):
            x = got[ids[2 + layer], t]
            for d in range(PLANE):
                out[d, t, layer] = x


def gather_kernel(ids, parts, out):
    out[...] = jnp.zeros_like(out)
    for layer in range(LAYERS):
        for t in range(2):
            x = [parts[d, t, layer] for d in range(PLANE)]
            while len(x) > 1:
                x = [a + b for a, b in zip(x[::2], x[1::2])]
            out[ids[2 + layer], t] = x[0]


def finish_kernel(got, out):
    for t in range(TILES):
        out[:, 128 * t:128 * (t + 1)] = got[t // 2, t % 2] + got[PLANE + t // 2, t % 2]


def vm():
    return pl.BlockSpec(memory_space=pltpu.VMEM)


def hbm():
    return pl.BlockSpec(memory_space=pltpu.HBM)


def in_hbm(x):
    return pltpu.with_memory_space_constraint(x, pltpu.HBM)


def sm():
    return pl.BlockSpec(memory_space=pltpu.SMEM)


def shape(*dims):
    return jax.ShapeDtypeStruct(dims, jnp.float32)


def field(rows):
    return shape(rows, 2, 128, 128)


def field_hbm(rows):
    return pltpu.HBM((rows, 2, 128, 128), jnp.float32)


def scr(*dims):
    return pltpu.VMEM(dims, jnp.float32)


def wide(rows):
    return scr(rows, 2, PAD, 128)


def call(kernel, ins, outs, scratch, mib, out_specs=None):
    return pl.pallas_call(
        kernel, out_shape=outs, in_specs=ins,
        out_specs=out_specs or jax.tree.map(lambda _: vm(), outs),
        scratch_shapes=scratch,
        compiler_params=pltpu.CompilerParams(vmem_limit_bytes=mib << 20),
        cost_estimate=pl.CostEstimate(flops=20_000_000, bytes_accessed=4 << 20, transcendentals=0),
    )


def forward_and_back(angles, depth_order, slices, cotangent):
    n_row = lax.axis_size("row")
    group = lax.axis_index("illum") // PLANE
    ids = jnp.concatenate(
        [jnp.stack([lax.axis_index("row"), group]).astype(jnp.int32), depth_order])
    groups = [list(range(g * PLANE, (g + 1) * PLANE)) for g in range(2)]

    def meet(x_e, x_o, by):
        even = [(i, i ^ by) for i in range(n_row)]
        odd = [(i, i + by) for i in range(by, n_row - by) if i & by]
        odd = odd + [(j, i) for i, j in odd]
        got_o = lax.ppermute(x_o, "row", odd)
        got_e = lax.ppermute(x_e, "row", even)
        return got_e, got_o

    def exchange(x, groups=groups):
        flat = x.reshape(-1, 128)
        flat = lax.all_to_all(flat, "illum", 0, 0, axis_index_groups=groups, tiled=True)
        return flat.reshape(x.shape)

    def rows_first(x):
        return x.reshape(8, ROWS, TILES, 128).transpose(0, 2, 1, 3).reshape(-1, 128)

    mine = slices[0].reshape(ROWS, TILES, 128).transpose(1, 0, 2)
    dealt = jnp.broadcast_to(mine[None], (2, TILES, ROWS, 128))
    dealt = dealt.reshape(2 * PLANE, 2, ROWS, 128)
    got = exchange(dealt, None)
    own, send_e, send_o = call(
        split_kernel, [sm(), vm()], (field_hbm(8), field(4), field(4)),
        [scr(8, 2, 128, 128), pltpu.SemaphoreType.DMA], 6, (hbm(), vm(), vm()))(
            ids, rows_first(cotangent))
    cot_e, cot_o = meet(send_e, send_o, 1)
    whole = call(pick_kernel, [sm(), vm()], shape(PLANE, 2, LAYERS, ROWS, 128), [],
                 2)(ids, got)
    phases = exchange(whole).reshape(-1, 128)
    w1 = call(
        adjoint_kernel, [sm(), hbm()] + [vm()] * 2, field_hbm(8),
        [scr(8, 2, 128, 128)] * 2 + [wide(16)] * 4 + [pltpu.SemaphoreType.DMA],
        14, hbm())(ids, in_hbm(own), cot_e, cot_o)
    ph_e, ph_o = meet(phases, phases, 1)
    w_e, w_o = meet(w1, w1, 1)

    table = scr(TILES * LAYERS * ROWS, 128)
    cos_own, sin_own = call(
        phase_kernel, [vm()], (shape(LAYERS * ROWS, 128, 128),) * 2, [table] * 2,
        5)(phases)
    *kept, last_e, last_o = call(
        forward_kernel, [sm()] * 2 + [vm()] * 4,
        (shape(LAYERS * EXT, 128, 128),) * 2 + (field(8),) * 3 + (field(4),) * 2,
        [table, table, scr(2, 128, 128)] + [wide(EXT)] * 5, 20)(
            ids, angles, ph_e, ph_o, cos_own, sin_own)
    terms = call(
        back_kernel, [sm()] + [vm()] * 8, shape(TILES * LAYERS * ROWS, 128),
        [wide(EXT)] * 2 + [scr(16, 2, 128, 128)] + [wide(EXT)] * 3, 21)(
            ids, *kept, w1, w_e, w_o)
    parts = exchange(terms).reshape(PLANE, 2, LAYERS, ROWS, 128)
    r_e, r_o = meet(last_e, last_o, 1)
    send = call(gather_kernel, [sm(), vm()], shape(2 * PLANE, 2, ROWS, 128), [],
                2)(ids, parts)
    back = exchange(send, None)
    out = call(exit_kernel, [sm()] + [vm()] * 4, shape(2048, 128),
               [wide(16)] * 4 + [scr(8, 2, 128, 128)], 12)(
                   ids, last_e, last_o, r_e, r_o)
    grad = call(finish_kernel, [vm()], shape(ROWS, COLS), [], 2)(back)
    out = out.reshape(8, TILES, ROWS, 128).transpose(0, 2, 1, 3)
    return out.reshape(cotangent.shape), grad[None]


def solution(mesh):
    placed = (P("illum", None), P(), P("illum", "row", None), P("illum", None, "row", None))
    return jax.shard_map(
        forward_and_back,
        mesh=mesh,
        in_specs=placed,
        out_specs=(P("illum", None, "row", None), P("illum", "row", None)),
        check_vma=False,
    )
```

profile of v0, /device:TPU:32, one launch (start us, length us, event | category | flops | bytes accessed | tf_op | source)
XLA Modules:
  0.0 116.8 jit_solution(15033700466107961200)
XLA Ops:
  0.6 0.0 copy-start.6
  0.7 0.7 pad_add_fusion.ids
  1.4 0.0 copy-start.1
  1.4 1.2 %copy-done.1 = f32[4,2,8,4096]{3,2,1,0:T(8,128)S(1)} copy-done((f32[4,2,8,4096]{3,2,1,0:T(8,128)S(1)}, f32[4,2,8,4096]{3,2,1,0:T(8,128)}, u32[]{:S(2)}) %copy-start.1) | copy-done | bytes 1048600
  2.6 2.3 %shard_map.63 = (f32[8,2,128,128]{3,2,1,0:T(8,128)}, f32[4,2,128,128]{3,2,1,0:T(8,128)S(1)}, f32[4,2,128,128]{3,2,1,0:T(8,128)S(1)}) custom-call(s32[5]{0:T(128)S(1)} %pad_add_fusion.ids, f32[2048,128]{1,0:T(8,128)S(1)} %bitcast.29), custom_call_target="tpu_custom_call" | custom-call | flops 20000000 | bytes 4194304 | tf_op jit(solution)/shard_map/pallas_call | solution.py:468
  5.0 0.1 collective-permute-start.4
  5.1 3.8 %collective-permute-start.5 = (f32[4,2,128,128]{3,2,1,0:T(8,128)S(1)}, f32[4,2,128,128]{3,2,1,0:T(8,128)S(1)}, u32[]{:S(2)}, u32[]{:S(2)}) collective-permute-start(f32[4,2,128,128]{3,2,1,0:T(8,128)S(1)} %get-tuple-element.25), channel_id=1, source_target_pairs={{1,2},{3,4},{5,6},{2,1},{4,3},{6,5},{9,10},{11,12},{13,14},{10,9},... | collective-permute-start | bytes 1572872 | tf_op jit(solution)/shard_map/ppermute | solution.py:452
  8.9 1.6 %broadcast_in_dim.4 = f32[2,32,8,128]{3,2,1,0:T(8,128)} broadcast(f32[32,8,128]{2,1,0:T(8,128)} %bitcast.33), dimensions={1,2,3} | broadcast | bytes 393216 | tf_op jit(solution)/shard_map/broadcast_in_dim | solution.py:465
  10.5 12.2 %all-to-all-start = ((f32[32,16,128]{2,1,0:T(8,128)}), f32[32,16,128]{2,1,0:T(8,128)S(1)}, u32[]{:S(2)}, u32[]{:S(2)}) async-start(f32[32,16,128]{2,1,0:T(8,128)} %bitcast.4), calls=%async_computation | async-start | bytes 524288 | tf_op jit(solution)/shard_map/all_to_all | solution.py:458
  22.7 0.0 collective-permute-done.4.got_e
  22.8 0.0 collective-permute-done.5.got_o
  22.8 4.7 %shard_map.64.w1 = f32[8,2,128,128]{3,2,1,0:T(8,128)} custom-call(s32[5]{0:T(128)S(1)} %pad_add_fusion.ids, f32[8,2,128,128]{3,2,1,0:T(8,128)} %get-tuple-element.23.own, f32[4,2,128,128]{3,2,1,0:T(8,128)S(1)} %collective-permute-done.4.got_e, f32[4,2,128,128]{3,2,1,0:T(8,128)S(1)} %collective-permute-done.5.got_o), custom_call_target="tpu_custom_call" | custom-call | flops 20000000 | bytes 4194304 | tf_op jit(solution)/shard_map/pallas_call | solution.py:476
  27.4 0.0 copy-start
  27.4 0.1 collective-permute-start.6
  27.5 2.4 %collective-permute-start.7 = (f32[8,2,128,128]{3,2,1,0:T(8,128)}, f32[8,2,128,128]{3,2,1,0:T(8,128)S(1)}, u32[]{:S(2)}, u32[]{:S(2)}) collective-permute-start(f32[8,2,128,128]{3,2,1,0:T(8,128)} %shard_map.64.w1), channel_id=1, source_target_pairs={{1,2},{3,4},{5,6},{2,1},{4,3},{6,5},{9,10},{11,12},{13,14},{10,9},... | collective-permute-start | bytes 3145736 | tf_op jit(solution)/shard_map/ppermute | solution.py:452
  30.0 7.9 %all-to-all-done = f32[32,16,128]{2,1,0:T(8,128)S(1)} async-done(((f32[32,16,128]{2,1,0:T(8,128)}), f32[32,16,128]{2,1,0:T(8,128)S(1)}, u32[]{:S(2)}, u32[]{:S(2)}) %all-to-all-start) | async-done | bytes 262176 | tf_op jit(solution)/shard_map/all_to_all | solution.py:458
  37.8 0.6 shard_map.59
  38.4 12.4 %all_to_all.38 = f32[16,48,128]{2,1,0:T(8,128)S(1)} all-to-all(f32[16,48,128]{2,1,0:T(8,128)S(1)} %bitcast.28), channel_id=1, replica_groups={{0,8,16,24,32,40,48,56,64,72,80,88,96,104,112,120},{128,136,144,152,160..., dimensions={0} | all-to-all | bytes 786432 | tf_op jit(solution)/shard_map/all_to_all | solution.py:458
  50.8 0.0 collective-permute-start
  50.8 1.9 %collective-permute-start.1 = (f32[768,128]{1,0:T(8,128)S(1)}, f32[768,128]{1,0:T(8,128)}, u32[]{:S(2)}, u32[]{:S(2)}) collective-permute-start(f32[768,128]{1,0:T(8,128)S(1)} %bitcast.26), channel_id=1, source_target_pairs={{1,2},{3,4},{5,6},{2,1},{4,3},{6,5},{9,10},{11,12},{13,14},{10,9},... | collective-permute-start | bytes 1179656 | tf_op jit(solution)/shard_map/ppermute | solution.py:452
  52.8 0.0 copy-done.6
  52.8 0.1 copy.6.angles
  52.9 2.1 %shard_map.60 = (f32[24,128,128]{2,1,0:T(8,128)S(1)}, f32[24,128,128]{2,1,0:T(8,128)S(1)}) custom-call(f32[768,128]{1,0:T(8,128)S(1)} %bitcast.27), custom_call_target="tpu_custom_call" | custom-call | flops 20000000 | bytes 4194304 | tf_op jit(solution)/shard_map/pallas_call | solution.py:484
  55.0 0.0 collective-permute-done.ph_e
  55.0 5.0 %collective-permute-done.1.ph_o = f32[768,128]{1,0:T(8,128)} collective-permute-done((f32[768,128]{1,0:T(8,128)S(1)}, f32[768,128]{1,0:T(8,128)}, u32[]{:S(2)}, u32[]{:S(2)}) %collective-permute-start.1) | collective-permute-done | bytes 393248 | tf_op jit(solution)/shard_map/ppermute | solution.py:452
  60.0 11.8 %shard_map.61 = (f32[72,128,128]{2,1,0:T(8,128)S(1)}, f32[72,128,128]{2,1,0:T(8,128)S(1)}, f32[8,2,128,128]{3,2,1,0:T(8,128)S(1)}, f32[8,2,128,128]{3,2,1,0:T(8,...) custom-call(s32[5]{0:T(128)S(1)} %pad_add_fusion.ids, ...), custom_call_target="tpu_custom_call" | custom-call | flops 20000000 | bytes 4194304 | tf_op jit(solution)/shard_map/pallas_call | solution.py:487
  71.9 0.0 copy-start.2
  71.9 0.0 copy-start.4
  71.9 0.0 collective-permute-done.6.w_e
  71.9 0.0 collective-permute-done.7.w_o
  71.9 0.0 copy-done
  71.9 8.1 %shard_map.65 = f32[768,128]{1,0:T(8,128)} custom-call(s32[5]{0:T(128)S(1)} %pad_add_fusion.ids, f32[72,128,128]{2,1,0:T(8,128)S(1)} %get-tuple-element.18.cosr, f32[72,128,128]{2,1,0:T(8,128)S(1)} %get-tuple-element.19.sinr, f32[8,2,128,128]{3,2,1,0:T(8,128)S(1)} %get-tuple-element.20.keep0, f32[8,2,128,128]{3,2,1,0:T(8,128)S(1)} %get-tuple-element.21.keep1, ...), custom_call_target="tpu_custom_call" | custom-call | flops 20000000 | bytes 4194304 | tf_op jit(solution)/shard_map/pallas_call | solution.py:492
  80.0 0.0 copy-done.2
  80.0 0.0 copy-done.4
  80.0 3.7 %all-to-all-start.2 = ((f32[16,48,128]{2,1,0:T(8,128)}), f32[16,48,128]{2,1,0:T(8,128)S(1)}, u32[]{:S(2)}, u32[]{:S(2)}) async-start(f32[16,48,128]{2,1,0:T(8,128)} %bitcast.14), calls=%async_computation.2 | async-start | bytes 786432 | tf_op jit(solution)/shard_map/all_to_all | solution.py:458
  83.7 0.5 collective-permute-start.2
  84.3 1.9 %collective-permute-start.3 = (f32[4,2,128,128]{3,2,1,0:T(8,128)}, f32[4,2,128,128]{3,2,1,0:T(8,128)S(1)}, u32[]{:S(2)}, u32[]{:S(2)}) collective-permute-start(f32[4,2,128,128]{3,2,1,0:T(8,128)} %copy-done.4), channel_id=1, source_target_pairs={{1,2},{3,4},{5,6},{2,1},{4,3},{6,5},{9,10},{11,12},{13,14},{10,9},... | collective-permute-start | bytes 1572872 | tf_op jit(solution)/shard_map/ppermute | solution.py:452
  86.2 8.2 %all-to-all-done.2 = f32[16,48,128]{2,1,0:T(8,128)S(1)} async-done(((f32[16,48,128]{2,1,0:T(8,128)}), f32[16,48,128]{2,1,0:T(8,128)S(1)}, u32[]{:S(2)}, u32[]{:S(2)}) %all-to-all-start.2) | async-done | bytes 393248 | tf_op jit(solution)/shard_map/all_to_all | solution.py:458
  94.4 1.3 %shard_map.66 = f32[32,2,8,128]{3,2,1,0:T(8,128)} custom-call(s32[5]{0:T(128)S(1)} %pad_add_fusion.ids, f32[16,2,3,8,128]{4,3,2,1,0:T(8,128)S(1)} %bitcast.24), custom_call_target="tpu_custom_call" | custom-call | flops 20000000 | bytes 4194304 | tf_op jit(solution)/shard_map/pallas_call | solution.py:498
  95.6 6.4 %all-to-all-start.3 = ((f32[32,16,128]{2,1,0:T(8,128)}), f32[32,16,128]{2,1,0:T(8,128)S(1)}, u32[]{:S(2)}, u32[]{:S(2)}) async-start(f32[32,16,128]{2,1,0:T(8,128)} %bitcast.16), calls=%async_computation.3 | async-start | bytes 524288 | tf_op jit(solution)/shard_map/all_to_all | solution.py:458
  102.1 0.0 collective-permute-done.2.got_e
  102.1 0.0 collective-permute-done.3.got_o
  102.1 0.0 copy-start.3
  102.1 1.0 copy-done.3
  103.1 1.0 copy-done.5
  104.2 4.3 %shard_map.62 = f32[2048,128]{1,0:T(8,128)} custom-call(s32[5]{0:T(128)S(1)} %pad_add_fusion.ids, f32[4,2,128,128]{3,2,1,0:T(8,128)S(1)} %copy-done.3, f32[4,2,128,128]{3,2,1,0:T(8,128)S(1)} %copy-done.5, f32[4,2,128,128]{3,2,1,0:T(8,128)S(1)} %collective-permute-done.2.got_e, f32[4,2,128,128]{3,2,1,0:T(8,128)S(1)} %collective-permute-done.3.got_o), custom_call_target="tpu_custom_call" | custom-call | flops 20000000 | bytes 4194304 | tf_op jit(solution)/shard_map/pallas_call | solution.py:501
  108.5 7.7 %all-to-all-done.3 = f32[32,16,128]{2,1,0:T(8,128)S(1)} async-done(((f32[32,16,128]{2,1,0:T(8,128)}), f32[32,16,128]{2,1,0:T(8,128)S(1)}, u32[]{:S(2)}, u32[]{:S(2)}) %all-to-all-start.3) | async-done | bytes 262176 | tf_op jit(solution)/shard_map/all_to_all | solution.py:458
  116.2 0.7 shard_map.67
  (1 shorter events, 0.0 us)
Async XLA Ops:
  0.6 52.1 %copy-start.6 = (s32[4,2]{0,1:T(2,128)S(1)}, s32[4,2]{0,1:T(2,128)}, u32[]{:S(2)}) copy-start(s32[4,2]{0,1:T(2,128)} %param.4) | copy-start | bytes 100
  1.4 1.2 %copy-start.1 = (f32[4,2,8,4096]{3,2,1,0:T(8,128)S(1)}, f32[4,2,8,4096]{3,2,1,0:T(8,128)}, u32[]{:S(2)}) copy-start(f32[4,2,8,4096]{3,2,1,0:T(8,128)} %param.7) | copy-start | bytes 3145732
  5.0 17.8 %collective-permute-start.4 = (f32[4,2,128,128]{3,2,1,0:T(8,128)S(1)}, f32[4,2,128,128]{3,2,1,0:T(8,128)S(1)}, u32[]{:S(2)}, u32[]{:S(2)}) collective-permute-start(f32[4,2,128,128]{3,2,1,0:T(8,128)S(1)} %get-tuple-element.24), channel_id=1, source_target_pairs={{0,1},{1,0},{2,3},{3,2},{4,5},{5,4},{6,7},{7,6},{8,9},{9,8},{10,11... | collective-permute-start | bytes 1572872 | tf_op jit(solution)/shard_map/ppermute | solution.py:453
  5.1 17.7 %collective-permute-start.5 = (f32[4,2,128,128]{3,2,1,0:T(8,128)S(1)}, f32[4,2,128,128]{3,2,1,0:T(8,128)S(1)}, u32[]{:S(2)}, u32[]{:S(2)}) collective-permute-start(f32[4,2,128,128]{3,2,1,0:T(8,128)S(1)} %get-tuple-element.25), channel_id=1, source_target_pairs={{1,2},{3,4},{5,6},{2,1},{4,3},{6,5},{9,10},{11,12},{13,14},{10,9},... | collective-permute-start | bytes 1572872 | tf_op jit(solution)/shard_map/ppermute | solution.py:452
  10.5 27.3 %all-to-all-start = ((f32[32,16,128]{2,1,0:T(8,128)}), f32[32,16,128]{2,1,0:T(8,128)S(1)}, u32[]{:S(2)}, u32[]{:S(2)}) async-start(f32[32,16,128]{2,1,0:T(8,128)} %bitcast.4), calls=%async_computation | async-start | bytes 524288 | tf_op jit(solution)/shard_map/all_to_all | solution.py:458
  27.4 44.5 %copy-start = (f32[8,2,128,128]{3,2,1,0:T(8,128)S(1)}, f32[8,2,128,128]{3,2,1,0:T(8,128)}, u32[]{:S(2)}) copy-start(f32[8,2,128,128]{3,2,1,0:T(8,128)} %shard_map.64.w1) | copy-start | bytes 3145732
  27.4 44.5 %collective-permute-start.6 = (f32[8,2,128,128]{3,2,1,0:T(8,128)}, f32[8,2,128,128]{3,2,1,0:T(8,128)S(1)}, u32[]{:S(2)}, u32[]{:S(2)}) collective-permute-start(f32[8,2,128,128]{3,2,1,0:T(8,128)} %shard_map.64.w1), channel_id=1, source_target_pairs={{0,1},{1,0},{2,3},{3,2},{4,5},{5,4},{6,7},{7,6},{8,9},{9,8},{10,11... | collective-permute-start | bytes 3145736 | tf_op jit(solution)/shard_map/ppermute | solution.py:453
  27.5 44.4 %collective-permute-start.7 = (f32[8,2,128,128]{3,2,1,0:T(8,128)}, f32[8,2,128,128]{3,2,1,0:T(8,128)S(1)}, u32[]{:S(2)}, u32[]{:S(2)}) collective-permute-start(f32[8,2,128,128]{3,2,1,0:T(8,128)} %shard_map.64.w1), channel_id=1, source_target_pairs={{1,2},{3,4},{5,6},{2,1},{4,3},{6,5},{9,10},{11,12},{13,14},{10,9},... | collective-permute-start | bytes 3145736 | tf_op jit(solution)/shard_map/ppermute | solution.py:452
  50.8 4.2 %collective-permute-start = (f32[768,128]{1,0:T(8,128)S(1)}, f32[768,128]{1,0:T(8,128)}, u32[]{:S(2)}, u32[]{:S(2)}) collective-permute-start(f32[768,128]{1,0:T(8,128)S(1)} %bitcast.25), channel_id=1, source_target_pairs={{0,1},{1,0},{2,3},{3,2},{4,5},{5,4},{6,7},{7,6},{8,9},{9,8},{10,11... | collective-permute-start | bytes 1179656 | tf_op jit(solution)/shard_map/ppermute | solution.py:453
  50.8 9.2 %collective-permute-start.1 = (f32[768,128]{1,0:T(8,128)S(1)}, f32[768,128]{1,0:T(8,128)}, u32[]{:S(2)}, u32[]{:S(2)}) collective-permute-start(f32[768,128]{1,0:T(8,128)S(1)} %bitcast.26), channel_id=1, source_target_pairs={{1,2},{3,4},{5,6},{2,1},{4,3},{6,5},{9,10},{11,12},{13,14},{10,9},... | collective-permute-start | bytes 1179656 | tf_op jit(solution)/shard_map/ppermute | solution.py:452
  71.9 8.1 %copy-start.2 = (f32[4,2,128,128]{3,2,1,0:T(8,128)}, f32[4,2,128,128]{3,2,1,0:T(8,128)S(1)}, u32[]{:S(2)}) copy-start(f32[4,2,128,128]{3,2,1,0:T(8,128)S(1)} %get-tuple-element.16.sent_e) | copy-start | bytes 1572868
  71.9 8.1 %copy-start.4 = (f32[4,2,128,128]{3,2,1,0:T(8,128)}, f32[4,2,128,128]{3,2,1,0:T(8,128)S(1)}, u32[]{:S(2)}) copy-start(f32[4,2,128,128]{3,2,1,0:T(8,128)S(1)} %get-tuple-element.17.sent_o) | copy-start | bytes 1572868
  80.0 14.4 %all-to-all-start.2 = ((f32[16,48,128]{2,1,0:T(8,128)}), f32[16,48,128]{2,1,0:T(8,128)S(1)}, u32[]{:S(2)}, u32[]{:S(2)}) async-start(f32[16,48,128]{2,1,0:T(8,128)} %bitcast.14), calls=%async_computation.2 | async-start | bytes 786432 | tf_op jit(solution)/shard_map/all_to_all | solution.py:458
  83.7 18.3 %collective-permute-start.2 = (f32[4,2,128,128]{3,2,1,0:T(8,128)}, f32[4,2,128,128]{3,2,1,0:T(8,128)S(1)}, u32[]{:S(2)}, u32[]{:S(2)}) collective-permute-start(f32[4,2,128,128]{3,2,1,0:T(8,128)} %copy-done.2), channel_id=1, source_target_pairs={{0,1},{1,0},{2,3},{3,2},{4,5},{5,4},{6,7},{7,6},{8,9},{9,8},{10,11... | collective-permute-start | bytes 1572872 | tf_op jit(solution)/shard_map/ppermute | solution.py:453
  84.3 17.8 %collective-permute-start.3 = (f32[4,2,128,128]{3,2,1,0:T(8,128)}, f32[4,2,128,128]{3,2,1,0:T(8,128)S(1)}, u32[]{:S(2)}, u32[]{:S(2)}) collective-permute-start(f32[4,2,128,128]{3,2,1,0:T(8,128)} %copy-done.4), channel_id=1, source_target_pairs={{1,2},{3,4},{5,6},{2,1},{4,3},{6,5},{9,10},{11,12},{13,14},{10,9},... | collective-permute-start | bytes 1572872 | tf_op jit(solution)/shard_map/ppermute | solution.py:452
  95.6 20.5 %all-to-all-start.3 = ((f32[32,16,128]{2,1,0:T(8,128)}), f32[32,16,128]{2,1,0:T(8,128)S(1)}, u32[]{:S(2)}, u32[]{:S(2)}) async-start(f32[32,16,128]{2,1,0:T(8,128)} %bitcast.16), calls=%async_computation.3 | async-start | bytes 524288 | tf_op jit(solution)/shard_map/all_to_all | solution.py:458
  102.1 1.0 copy-start.3
  103.1 1.0 copy-start.5
where the time goes:
time: 118 us; the launch traced here: 117 us
  Pallas kernels  35.9 us (30%)
  starting transfers between devices  33.1 us (28%)
  waiting for transfers between devices  28.8 us (24%)
  blocking collectives  12.4 us (11%)
  local copies, waits for them, and re-layouts  5.03 us (4%)
    all_to_all x3, waiting for transfers between devices, exchange(): lax.all_to_all(flat, 'illum', 0, 0, axis_index_groups=groups, tiled=True)  23.7 us
    all_to_all x3, starting transfers between devices, exchange(): lax.all_to_all(flat, 'illum', 0, 0, axis_index_groups=groups, tiled=True)  22.4 us
    all_to_all x1, blocking collectives, exchange(): lax.all_to_all(flat, 'illum', 0, 0, axis_index_groups=groups, tiled=True)  12.4 us
    pallas_call x1, Pallas kernels, forward_and_back(): call(forward_kernel, [sm()] * 2 + [vm()] * 4, (shape(LAYERS * EXT, 128, 1...  11.8 us
    ppermute x4, starting transfers between devices, meet(): got_o = lax.ppermute(x_o, 'row', odd)  10 us
    pallas_call x1, Pallas kernels, forward_and_back(): call(back_kernel, [sm()] + [vm()] * 8, shape(TILES * LAYERS * ROWS, 128),...  8.07 us
    ppermute x4, waiting for transfers between devices, meet(): got_o = lax.ppermute(x_o, 'row', odd)  5.04 us
    pallas_call x1, Pallas kernels, forward_and_back(): call(adjoint_kernel, [sm(), hbm()] + [vm()] * 2, field_hbm(8), [scr(8, 2,...  4.66 us
  transfers between devices with their start and end apart: 11, of which 4 were waited for; matrix products, arithmetic and copies ran while one was open for 1% of the time, Pallas kernels for 21%

commit v1 on v0

--- a/solution.py
+++ b/solution.py
@@ -68,10 +68,10 @@
             ref[at] = jnp.zeros((2, PAD, 128), jnp.float32)
 
 
-def lap_pair(src, r, k, j):
-    v = [src[r + q, k, padded(j), :] for q in (-1, 0, 1, 2)]
+def lap_rows(src, r, n, k, j):
+    v = [src[r + q, k, padded(j), :] for q in range(-1, n + 1)]
     out = []
-    for q in (0, 1):
+    for q in range(n):
         side = src[r + q, k, padded(j, -1), :] + src[r + q, k, padded(j, 1), :]
         out.append((v[q] + v[q + 2]) + side - 4.0 * v[q + 1])
     return out
@@ -82,16 +82,19 @@
     for n, dst in enumerate(powers):
         lo, count = base - h + 1 + n, ROWS + 2 * (h - 1 - n)
 
-        def body(i, _, prev=prev, dst=dst, lo=lo):
-            r = lo + 2 * i
+        def body(r, n, prev=prev, dst=dst):
             for k in range(2):
                 for j in range(16):
-                    pair = lap_pair(prev, r, k, j)
-                    for q in (0, 1):
-                        dst[r + q, k, padded(j), :] = pair[q]
+                    for q, x in enumerate(lap_rows(prev, r, n, k, j)):
+                        dst[r + q, k, padded(j), :] = x
+
+        def four(i, _, body=body, lo=lo):
+            body(lo + 4 * i, 4)
             return 0
 
-        lax.fori_loop(0, count // 2, body, 0)
+        lax.fori_loop(0, count // 4, four, 0)
+        if count % 4:
+            body(lo + count - 2, 2)
         fill_pads(dst, rows)
         clear_outside(row, dst, base, rows)
         prev = dst
@@ -102,7 +105,7 @@
     def last(i, _):
         r = lo + 2 * i
         for j in range(16):
-            l4 = [lap_pair(l3, r, k, j) for k in range(2)]
+            l4 = [lap_rows(l3, r, 2, k, j) for k in range(2)]
             for q in (0, 1):
                 even, odd = [], []
                 for k in range(2):
@@ -169,13 +172,21 @@
     give.wait()
 
 
-def exit_kernel(ids, sent_e, sent_o, got_e, got_o, out, u, l1, l2, l3, res):
+def exit_kernel(ids, sent_e, sent_o, got_e, got_o, out, u, l1, l2, l3, res, held, sems):
     row = ids[0]
     odd = row & 1
-    put(u, 8 - 4 * odd, sent_e, 4)
-    put(u, 4 + 4 * odd, sent_o, 4)
+    fetch = [
+        pltpu.make_async_copy(src, held.at[n], sems.at[n])
+        for n, src in enumerate((sent_e, sent_o))
+    ]
+    for c in fetch:
+        c.start()
     put(u, 12 - 12 * odd, got_e, 4)
     put(u, 12 * odd, got_o, 4)
+    fetch[0].wait()
+    put(u, 8 - 4 * odd, held.at[0], 4)
+    fetch[1].wait()
+    put(u, 4 + 4 * odd, held.at[1], 4)
     fill_pads(u, 16)
 
     def write(r, j, re, im):
@@ -224,7 +235,7 @@
 
 def forward_kernel(ids, angles, ph_e, ph_o, cos_own, sin_own,
                    cosr, sinr, keep0, keep1, keep2, last_e, last_o,
-                   cos_n, sin_n, beam, u, v, l1, l2, l3):
+                   cos_n, sin_n, beam, u, v, l1, l2, l3, sems):
     row = ids[0]
     odd = row & 1
     for ph, above in ((ph_e, odd), (ph_o, 1 - odd)):
@@ -267,19 +278,20 @@
 
     phase_at = functools.partial(rotation, cosr, sinr)
 
-    def incident(r, _):
-        k = (pv * (row * ROWS + r - HALO)) & (NX - 1)
-        sa, ca = sincos((k - NX // 2).astype(jnp.float32) * (2.0 * math.pi / NX))
-        for j in range(16):
-            c, s = phase_at(0, r, j)
-            a = sa * s - ca * c
-            b = -(sa * c + ca * s)
-            er, ei = beam[0, chunk(j), :], beam[1, chunk(j), :]
-            u[r, 0, padded(j), :] = er * a - ei * b
-            u[r, 1, padded(j), :] = ei * a + er * b
-        return 0
-
-    lax.fori_loop(0, EXT, incident, 0)
+    def incident(i, _):
+        for r in (2 * i, 2 * i + 1):
+            k = (pv * (row * ROWS + r - HALO)) & (NX - 1)
+            sa, ca = sincos((k - NX // 2).astype(jnp.float32) * (2.0 * math.pi / NX))
+            for j in range(16):
+                c, s = phase_at(0, r, j)
+                a = sa * s - ca * c
+                b = -(sa * c + ca * s)
+                er, ei = beam[0, chunk(j), :], beam[1, chunk(j), :]
+                u[r, 0, padded(j), :] = er * a - ei * b
+                u[r, 1, padded(j), :] = ei * a + er * b
+        return 0
+
+    lax.fori_loop(0, EXT // 2, incident, 0)
     fill_pads(u, EXT)
     clear_outside(row, u, HALO, EXT)
 
@@ -298,6 +310,12 @@
         keep2[r - HALO, 1, chunk(j), :] = re * s + im * c
 
     step(row, v, EXT, HALO, 4, (l1, l2, l3), rate_scale, write_last)
+    give = [
+        pltpu.make_async_copy(keep2.at[pl.ds(at, 4)], dst, sems.at[n])
+        for n, (at, dst) in enumerate(((4 * (1 - odd), last_e), (4 * odd, last_o)))
+    ]
+    for c in give:
+        c.start()
 
     def keep(r, _):
         for k in range(2):
@@ -306,9 +324,8 @@
         return 0
 
     lax.fori_loop(0, ROWS, keep, 0)
-    for r in range(4):
-        last_e[r] = keep2[r + 4 * (1 - odd)]
-        last_o[r] = keep2[r + 4 * odd]
+    for c in give:
+        c.wait()
 
 
 def rotation(cosr, sinr, layer, r, j):
@@ -369,6 +386,17 @@
     term(0, of(raw, 4), of(keep0))
 
 
+def double_kernel(mine, out, held, sems):
+    fetch = pltpu.make_async_copy(mine, held, sems.at[0])
+    fetch.start()
+    fetch.wait()
+    give = [pltpu.make_async_copy(held, out.at[n], sems.at[n]) for n in range(2)]
+    for c in give:
+        c.start()
+    for c in give:
+        c.wait()
+
+
 def pick_kernel(ids, got, out):
     for layer in range(LAYERS):
         for t in range(2):
@@ -462,7 +490,9 @@
         return x.reshape(8, ROWS, TILES, 128).transpose(0, 2, 1, 3).reshape(-1, 128)
 
     mine = slices[0].reshape(ROWS, TILES, 128).transpose(1, 0, 2)
-    dealt = jnp.broadcast_to(mine[None], (2, TILES, ROWS, 128))
+    dealt = call(double_kernel, [hbm()], pltpu.HBM((2, TILES, ROWS, 128), jnp.float32),
+                 [scr(TILES, ROWS, 128), pltpu.SemaphoreType.DMA((2,))], 2, hbm())(
+                     in_hbm(mine))
     dealt = dealt.reshape(2 * PLANE, 2, ROWS, 128)
     got = exchange(dealt, None)
     own, send_e, send_o = call(
@@ -486,8 +516,9 @@
         5)(phases)
     *kept, last_e, last_o = call(
         forward_kernel, [sm()] * 2 + [vm()] * 4,
-        (shape(LAYERS * EXT, 128, 128),) * 2 + (field(8),) * 3 + (field(4),) * 2,
-        [table, table, scr(2, 128, 128)] + [wide(EXT)] * 5, 20)(
+        (shape(LAYERS * EXT, 128, 128),) * 2 + (field(8),) * 3 + (field_hbm(4),) * 2,
+        [table, table, scr(2, 128, 128)] + [wide(EXT)] * 5
+        + [pltpu.SemaphoreType.DMA((2,))], 20, (vm(),) * 5 + (hbm(),) * 2)(
             ids, angles, ph_e, ph_o, cos_own, sin_own)
     terms = call(
         back_kernel, [sm()] + [vm()] * 8, shape(TILES * LAYERS * ROWS, 128),
@@ -498,9 +529,10 @@
     send = call(gather_kernel, [sm(), vm()], shape(2 * PLANE, 2, ROWS, 128), [],
                 2)(ids, parts)
     back = exchange(send, None)
-    out = call(exit_kernel, [sm()] + [vm()] * 4, shape(2048, 128),
-               [wide(16)] * 4 + [scr(8, 2, 128, 128)], 12)(
-                   ids, last_e, last_o, r_e, r_o)
+    out = call(exit_kernel, [sm()] + [hbm()] * 2 + [vm()] * 2, shape(2048, 128),
+               [wide(16)] * 4 + [scr(8, 2, 128, 128), scr(2, 4, 2, 128, 128),
+                                 pltpu.SemaphoreType.DMA((2,))], 13)(
+                   ids, in_hbm(last_e), in_hbm(last_o), r_e, r_o)
     grad = call(finish_kernel, [vm()], shape(ROWS, COLS), [], 2)(back)
     out = out.reshape(8, TILES, ROWS, 128).transpose(0, 2, 1, 3)
     return out.reshape(cotangent.shape), grad[None]

time: 118 us -> 117 us (level)
  local copies, waits for them, and re-layouts: 5.03 us -> 1.33 us
  Pallas kernels: 35.9 us -> 37.4 us
  waiting for transfers between devices: 28.8 us -> 30.3 us
    pallas_call x1 -> x2, Pallas kernels: 4.32 us -> 6.78 us  [the longest x1 5.14 us: forward_and_back(): call(exit_kernel, [sm()] + [hbm()] * 2 + [vm()] * 2, shape(2048, 128), [w...]
    unnamed x15 -> x7, local copies, waits for them, and re-layouts: 3.42 us -> 1.33 us
    broadcast_in_dim x1 -> x0, local copies, waits for them, and re-layouts: 1.61 us -> none  [forward_and_back(): dealt = jnp.broadcast_to(mine[None], (2, TILES, ROWS, 128))]
    all_to_all x3, waiting for transfers between devices: 23.7 us -> 25.3 us  [exchange(): lax.all_to_all(flat, 'illum', 0, 0, axis_index_groups=groups, tiled=True)]
  transfers between devices with their start and end apart: 11 -> 11, of which waited for: 4 -> 4; matrix products, arithmetic and copies ran while one was open for 1% -> 0% of each run, Pallas kernels for 21% -> 23%
where the time goes in v1:
time: 117 us; the launch traced here: 116 us
  Pallas kernels  37.4 us (32%)
  starting transfers between devices  32.9 us (28%)
  waiting for transfers between devices  30.3 us (26%)
  blocking collectives  12.4 us (11%)
  local copies, waits for them, and re-layouts  1.33 us (1%)
    all_to_all x3, waiting for transfers between devices, exchange(): lax.all_to_all(flat, 'illum', 0, 0, axis_index_groups=groups, tiled=True)  25.3 us
    all_to_all x3, starting transfers between devices, exchange(): lax.all_to_all(flat, 'illum', 0, 0, axis_index_groups=groups, tiled=True)  22.1 us
    all_to_all x1, blocking collectives, exchange(): lax.all_to_all(flat, 'illum', 0, 0, axis_index_groups=groups, tiled=True)  12.4 us
    pallas_call x1, Pallas kernels, forward_and_back(): call(forward_kernel, [sm()] * 2 + [vm()] * 4, (shape(LAYERS * EXT, 128, 1...  11.7 us
    ppermute x4, starting transfers between devices, meet(): got_o = lax.ppermute(x_o, 'row', odd)  10 us
    pallas_call x1, Pallas kernels, forward_and_back(): call(back_kernel, [sm()] + [vm()] * 8, shape(TILES * LAYERS * ROWS, 128),...  7.55 us
    pallas_call x1, Pallas kernels, forward_and_back(): call(exit_kernel, [sm()] + [hbm()] * 2 + [vm()] * 2, shape(2048, 128), [w...  5.14 us
    ppermute x4, waiting for transfers between devices, meet(): got_o = lax.ppermute(x_o, 'row', odd)  5.04 us
  transfers between devices with their start and end apart: 11, of which 4 were waited for; matrix products, arithmetic and copies ran while one was open for 0% of the time, Pallas kernels for 23%

profile of v1, /device:TPU:32, one launch (start us, length us, event | category | flops | bytes accessed | tf_op | source)
XLA Modules:
  0.0 116.0 jit_solution(1176907835624024040)
XLA Ops:
  0.6 0.0 copy-start.2
  0.7 0.7 pad_add_fusion.ids
  1.4 0.0 copy-start.1
  1.4 1.2 %copy-done.1 = f32[4,2,8,4096]{3,2,1,0:T(8,128)S(1)} copy-done((f32[4,2,8,4096]{3,2,1,0:T(8,128)S(1)}, f32[4,2,8,4096]{3,2,1,0:T(8,128)}, u32[]{:S(2)}) %copy-start.1) | copy-done | bytes 1048600
  2.6 2.3 %shard_map.64 = (f32[8,2,128,128]{3,2,1,0:T(8,128)}, f32[4,2,128,128]{3,2,1,0:T(8,128)S(1)}, f32[4,2,128,128]{3,2,1,0:T(8,128)S(1)}) custom-call(s32[5]{0:T(128)S(1)} %pad_add_fusion.ids, f32[2048,128]{1,0:T(8,128)S(1)} %bitcast.29), custom_call_target="tpu_custom_call" | custom-call | flops 20000000 | bytes 4194304 | tf_op jit(solution)/shard_map/pallas_call | solution.py:498
  5.0 0.1 collective-permute-start.4
  5.1 3.8 %collective-permute-start.5 = (f32[4,2,128,128]{3,2,1,0:T(8,128)S(1)}, f32[4,2,128,128]{3,2,1,0:T(8,128)S(1)}, u32[]{:S(2)}, u32[]{:S(2)}) collective-permute-start(f32[4,2,128,128]{3,2,1,0:T(8,128)S(1)} %get-tuple-element.25), channel_id=1, source_target_pairs={{1,2},{3,4},{5,6},{2,1},{4,3},{6,5},{9,10},{11,12},{13,14},{10,9},... | collective-permute-start | bytes 1572872 | tf_op jit(solution)/shard_map/ppermute | solution.py:480
  8.9 1.6 %shard_map.59 = f32[2,32,8,128]{3,2,1,0:T(8,128)} custom-call(f32[32,8,128]{2,1,0:T(8,128)} %bitcast.34), custom_call_target="tpu_custom_call" | custom-call | flops 20000000 | bytes 4194304 | tf_op jit(solution)/shard_map/pallas_call | solution.py:493
  10.5 12.2 %all-to-all-start = ((f32[32,16,128]{2,1,0:T(8,128)}), f32[32,16,128]{2,1,0:T(8,128)S(1)}, u32[]{:S(2)}, u32[]{:S(2)}) async-start(f32[32,16,128]{2,1,0:T(8,128)} %bitcast.33), calls=%async_computation | async-start | bytes 524288 | tf_op jit(solution)/shard_map/all_to_all | solution.py:486
  22.8 0.0 collective-permute-done.4.got_e
  22.8 0.0 collective-permute-done.5.got_o
  22.8 4.4 %shard_map.65.w1 = f32[8,2,128,128]{3,2,1,0:T(8,128)} custom-call(s32[5]{0:T(128)S(1)} %pad_add_fusion.ids, f32[8,2,128,128]{3,2,1,0:T(8,128)} %get-tuple-element.23.own, f32[4,2,128,128]{3,2,1,0:T(8,128)S(1)} %collective-permute-done.4.got_e, f32[4,2,128,128]{3,2,1,0:T(8,128)S(1)} %collective-permute-done.5.got_o), custom_call_target="tpu_custom_call" | custom-call | flops 20000000 | bytes 4194304 | tf_op jit(solution)/shard_map/pallas_call | solution.py:506
  27.2 0.0 copy-start
  27.2 0.1 collective-permute-start.6
  27.3 2.4 %collective-permute-start.7 = (f32[8,2,128,128]{3,2,1,0:T(8,128)}, f32[8,2,128,128]{3,2,1,0:T(8,128)S(1)}, u32[]{:S(2)}, u32[]{:S(2)}) collective-permute-start(f32[8,2,128,128]{3,2,1,0:T(8,128)} %shard_map.65.w1), channel_id=1, source_target_pairs={{1,2},{3,4},{5,6},{2,1},{4,3},{6,5},{9,10},{11,12},{13,14},{10,9},... | collective-permute-start | bytes 3145736 | tf_op jit(solution)/shard_map/ppermute | solution.py:480
  29.7 8.1 %all-to-all-done = f32[32,16,128]{2,1,0:T(8,128)S(1)} async-done(((f32[32,16,128]{2,1,0:T(8,128)}), f32[32,16,128]{2,1,0:T(8,128)S(1)}, u32[]{:S(2)}, u32[]{:S(2)}) %all-to-all-start) | async-done | bytes 262176 | tf_op jit(solution)/shard_map/all_to_all | solution.py:486
  37.9 0.6 shard_map.60
  38.5 12.4 %all_to_all.38 = f32[16,48,128]{2,1,0:T(8,128)S(1)} all-to-all(f32[16,48,128]{2,1,0:T(8,128)S(1)} %bitcast.28), channel_id=1, replica_groups={{0,8,16,24,32,40,48,56,64,72,80,88,96,104,112,120},{128,136,144,152,160..., dimensions={0} | all-to-all | bytes 786432 | tf_op jit(solution)/shard_map/all_to_all | solution.py:486
  50.9 0.0 collective-permute-start
  50.9 1.9 %collective-permute-start.1 = (f32[768,128]{1,0:T(8,128)S(1)}, f32[768,128]{1,0:T(8,128)}, u32[]{:S(2)}, u32[]{:S(2)}) collective-permute-start(f32[768,128]{1,0:T(8,128)S(1)} %bitcast.26), channel_id=1, source_target_pairs={{1,2},{3,4},{5,6},{2,1},{4,3},{6,5},{9,10},{11,12},{13,14},{10,9},... | collective-permute-start | bytes 1179656 | tf_op jit(solution)/shard_map/ppermute | solution.py:480
  52.8 0.0 copy-done.2
  52.8 0.1 copy.6.angles
  52.9 2.1 %shard_map.61 = (f32[24,128,128]{2,1,0:T(8,128)S(1)}, f32[24,128,128]{2,1,0:T(8,128)S(1)}) custom-call(f32[768,128]{1,0:T(8,128)S(1)} %bitcast.27), custom_call_target="tpu_custom_call" | custom-call | flops 20000000 | bytes 4194304 | tf_op jit(solution)/shard_map/pallas_call | solution.py:514
  55.0 0.0 collective-permute-done.ph_e
  55.1 5.0 %collective-permute-done.1.ph_o = f32[768,128]{1,0:T(8,128)} collective-permute-done((f32[768,128]{1,0:T(8,128)S(1)}, f32[768,128]{1,0:T(8,128)}, u32[]{:S(2)}, u32[]{:S(2)}) %collective-permute-start.1) | collective-permute-done | bytes 393248 | tf_op jit(solution)/shard_map/ppermute | solution.py:480
  60.1 11.7 %shard_map.62 = (f32[72,128,128]{2,1,0:T(8,128)S(1)}, f32[72,128,128]{2,1,0:T(8,128)S(1)}, f32[8,2,128,128]{3,2,1,0:T(8,128)S(1)}, f32[8,2,128,128]{3,2,1,0:T(8,...) custom-call(s32[5]{0:T(128)S(1)} %pad_add_fusion.ids, ...), custom_call_target="tpu_custom_call" | custom-call | flops 20000000 | bytes 4194304 | tf_op jit(solution)/shard_map/pallas_call | solution.py:517
  71.8 0.0 collective-permute-done.6.w_e
  71.8 0.0 collective-permute-done.7.w_o
  71.9 0.0 copy-done
  71.9 7.6 %shard_map.66 = f32[768,128]{1,0:T(8,128)} custom-call(s32[5]{0:T(128)S(1)} %pad_add_fusion.ids, f32[72,128,128]{2,1,0:T(8,128)S(1)} %get-tuple-element.18.cosr, f32[72,128,128]{2,1,0:T(8,128)S(1)} %get-tuple-element.19.sinr, f32[8,2,128,128]{3,2,1,0:T(8,128)S(1)} %get-tuple-element.20.keep0, f32[8,2,128,128]{3,2,1,0:T(8,128)S(1)} %get-tuple-element.21.keep1, ...), custom_call_target="tpu_custom_call" | custom-call | flops 20000000 | bytes 4194304 | tf_op jit(solution)/shard_map/pallas_call | solution.py:523
  79.4 3.7 %all-to-all-start.2 = ((f32[16,48,128]{2,1,0:T(8,128)}), f32[16,48,128]{2,1,0:T(8,128)S(1)}, u32[]{:S(2)}, u32[]{:S(2)}) async-start(f32[16,48,128]{2,1,0:T(8,128)} %bitcast.14), calls=%async_computation.2 | async-start | bytes 786432 | tf_op jit(solution)/shard_map/all_to_all | solution.py:486
  83.1 0.6 collective-permute-start.2
  83.7 1.9 %collective-permute-start.3 = (f32[4,2,128,128]{3,2,1,0:T(8,128)}, f32[4,2,128,128]{3,2,1,0:T(8,128)S(1)}, u32[]{:S(2)}, u32[]{:S(2)}) collective-permute-start(f32[4,2,128,128]{3,2,1,0:T(8,128)} %get-tuple-element.17.sent_o), channel_id=1, source_target_pairs={{1,2},{3,4},{5,6},{2,1},{4,3},{6,5},{9,10},{11,12},{13,14},{10,9},... | collective-permute-start | bytes 1572872 | tf_op jit(solution)/shard_map/ppermute | solution.py:480
  85.6 8.2 %all-to-all-done.2 = f32[16,48,128]{2,1,0:T(8,128)S(1)} async-done(((f32[16,48,128]{2,1,0:T(8,128)}), f32[16,48,128]{2,1,0:T(8,128)S(1)}, u32[]{:S(2)}, u32[]{:S(2)}) %all-to-all-start.2) | async-done | bytes 393248 | tf_op jit(solution)/shard_map/all_to_all | solution.py:486
  93.8 1.3 %shard_map.67 = f32[32,2,8,128]{3,2,1,0:T(8,128)} custom-call(s32[5]{0:T(128)S(1)} %pad_add_fusion.ids, f32[16,2,3,8,128]{4,3,2,1,0:T(8,128)S(1)} %bitcast.24), custom_call_target="tpu_custom_call" | custom-call | flops 20000000 | bytes 4194304 | tf_op jit(solution)/shard_map/pallas_call | solution.py:529
  95.1 6.1 %all-to-all-start.3 = ((f32[32,16,128]{2,1,0:T(8,128)}), f32[32,16,128]{2,1,0:T(8,128)S(1)}, u32[]{:S(2)}, u32[]{:S(2)}) async-start(f32[32,16,128]{2,1,0:T(8,128)} %bitcast.16), calls=%async_computation.3 | async-start | bytes 524288 | tf_op jit(solution)/shard_map/all_to_all | solution.py:486
  101.2 0.0 collective-permute-done.2.got_e
  101.2 0.0 collective-permute-done.3.got_o
  101.2 5.1 %shard_map.63 = f32[2048,128]{1,0:T(8,128)} custom-call(s32[5]{0:T(128)S(1)} %pad_add_fusion.ids, f32[4,2,128,128]{3,2,1,0:T(8,128)} %get-tuple-element.16.sent_e, f32[4,2,128,128]{3,2,1,0:T(8,128)} %get-tuple-element.17.sent_o, f32[4,2,128,128]{3,2,1,0:T(8,128)S(1)} %collective-permute-done.2.got_e, f32[4,2,128,128]{3,2,1,0:T(8,128)S(1)} %collective-permute-done.3.got_o), custom_call_target="tpu_custom_call" | custom-call | flops 20000000 | bytes 4194304 | tf_op jit(solution)/shard_map/pallas_call | solution.py:532
  106.4 8.9 %all-to-all-done.3 = f32[32,16,128]{2,1,0:T(8,128)S(1)} async-done(((f32[32,16,128]{2,1,0:T(8,128)}), f32[32,16,128]{2,1,0:T(8,128)S(1)}, u32[]{:S(2)}, u32[]{:S(2)}) %all-to-all-start.3) | async-done | bytes 262176 | tf_op jit(solution)/shard_map/all_to_all | solution.py:486
  115.3 0.7 shard_map.68
Async XLA Ops:
  0.6 52.2 %copy-start.2 = (s32[4,2]{0,1:T(2,128)S(1)}, s32[4,2]{0,1:T(2,128)}, u32[]{:S(2)}) copy-start(s32[4,2]{0,1:T(2,128)} %param.4) | copy-start | bytes 100
  1.4 1.2 %copy-start.1 = (f32[4,2,8,4096]{3,2,1,0:T(8,128)S(1)}, f32[4,2,8,4096]{3,2,1,0:T(8,128)}, u32[]{:S(2)}) copy-start(f32[4,2,8,4096]{3,2,1,0:T(8,128)} %param.7) | copy-start | bytes 3145732
  5.0 17.8 %collective-permute-start.4 = (f32[4,2,128,128]{3,2,1,0:T(8,128)S(1)}, f32[4,2,128,128]{3,2,1,0:T(8,128)S(1)}, u32[]{:S(2)}, u32[]{:S(2)}) collective-permute-start(f32[4,2,128,128]{3,2,1,0:T(8,128)S(1)} %get-tuple-element.24), channel_id=1, source_target_pairs={{0,1},{1,0},{2,3},{3,2},{4,5},{5,4},{6,7},{7,6},{8,9},{9,8},{10,11... | collective-permute-start | bytes 1572872 | tf_op jit(solution)/shard_map/ppermute | solution.py:481
  5.1 17.7 %collective-permute-start.5 = (f32[4,2,128,128]{3,2,1,0:T(8,128)S(1)}, f32[4,2,128,128]{3,2,1,0:T(8,128)S(1)}, u32[]{:S(2)}, u32[]{:S(2)}) collective-permute-start(f32[4,2,128,128]{3,2,1,0:T(8,128)S(1)} %get-tuple-element.25), channel_id=1, source_target_pairs={{1,2},{3,4},{5,6},{2,1},{4,3},{6,5},{9,10},{11,12},{13,14},{10,9},... | collective-permute-start | bytes 1572872 | tf_op jit(solution)/shard_map/ppermute | solution.py:480
  10.5 27.3 %all-to-all-start = ((f32[32,16,128]{2,1,0:T(8,128)}), f32[32,16,128]{2,1,0:T(8,128)S(1)}, u32[]{:S(2)}, u32[]{:S(2)}) async-start(f32[32,16,128]{2,1,0:T(8,128)} %bitcast.33), calls=%async_computation | async-start | bytes 524288 | tf_op jit(solution)/shard_map/all_to_all | solution.py:486
  27.2 44.6 %copy-start = (f32[8,2,128,128]{3,2,1,0:T(8,128)S(1)}, f32[8,2,128,128]{3,2,1,0:T(8,128)}, u32[]{:S(2)}) copy-start(f32[8,2,128,128]{3,2,1,0:T(8,128)} %shard_map.65.w1) | copy-start | bytes 3145732
  27.2 44.6 %collective-permute-start.6 = (f32[8,2,128,128]{3,2,1,0:T(8,128)}, f32[8,2,128,128]{3,2,1,0:T(8,128)S(1)}, u32[]{:S(2)}, u32[]{:S(2)}) collective-permute-start(f32[8,2,128,128]{3,2,1,0:T(8,128)} %shard_map.65.w1), channel_id=1, source_target_pairs={{0,1},{1,0},{2,3},{3,2},{4,5},{5,4},{6,7},{7,6},{8,9},{9,8},{10,11... | collective-permute-start | bytes 3145736 | tf_op jit(solution)/shard_map/ppermute | solution.py:481
  27.3 44.5 %collective-permute-start.7 = (f32[8,2,128,128]{3,2,1,0:T(8,128)}, f32[8,2,128,128]{3,2,1,0:T(8,128)S(1)}, u32[]{:S(2)}, u32[]{:S(2)}) collective-permute-start(f32[8,2,128,128]{3,2,1,0:T(8,128)} %shard_map.65.w1), channel_id=1, source_target_pairs={{1,2},{3,4},{5,6},{2,1},{4,3},{6,5},{9,10},{11,12},{13,14},{10,9},... | collective-permute-start | bytes 3145736 | tf_op jit(solution)/shard_map/ppermute | solution.py:480
  50.9 4.2 %collective-permute-start = (f32[768,128]{1,0:T(8,128)S(1)}, f32[768,128]{1,0:T(8,128)}, u32[]{:S(2)}, u32[]{:S(2)}) collective-permute-start(f32[768,128]{1,0:T(8,128)S(1)} %bitcast.25), channel_id=1, source_target_pairs={{0,1},{1,0},{2,3},{3,2},{4,5},{5,4},{6,7},{7,6},{8,9},{9,8},{10,11... | collective-permute-start | bytes 1179656 | tf_op jit(solution)/shard_map/ppermute | solution.py:481
  50.9 9.2 %collective-permute-start.1 = (f32[768,128]{1,0:T(8,128)S(1)}, f32[768,128]{1,0:T(8,128)}, u32[]{:S(2)}, u32[]{:S(2)}) collective-permute-start(f32[768,128]{1,0:T(8,128)S(1)} %bitcast.26), channel_id=1, source_target_pairs={{1,2},{3,4},{5,6},{2,1},{4,3},{6,5},{9,10},{11,12},{13,14},{10,9},... | collective-permute-start | bytes 1179656 | tf_op jit(solution)/shard_map/ppermute | solution.py:480
  79.4 14.4 %all-to-all-start.2 = ((f32[16,48,128]{2,1,0:T(8,128)}), f32[16,48,128]{2,1,0:T(8,128)S(1)}, u32[]{:S(2)}, u32[]{:S(2)}) async-start(f32[16,48,128]{2,1,0:T(8,128)} %bitcast.14), calls=%async_computation.2 | async-start | bytes 786432 | tf_op jit(solution)/shard_map/all_to_all | solution.py:486
  83.1 18.0 %collective-permute-start.2 = (f32[4,2,128,128]{3,2,1,0:T(8,128)}, f32[4,2,128,128]{3,2,1,0:T(8,128)S(1)}, u32[]{:S(2)}, u32[]{:S(2)}) collective-permute-start(f32[4,2,128,128]{3,2,1,0:T(8,128)} %get-tuple-element.16.sent_e), channel_id=1, source_target_pairs={{0,1},{1,0},{2,3},{3,2},{4,5},{5,4},{6,7},{7,6},{8,9},{9,8},{10,11... | collective-permute-start | bytes 1572872 | tf_op jit(solution)/shard_map/ppermute | solution.py:481
  83.7 17.5 %collective-permute-start.3 = (f32[4,2,128,128]{3,2,1,0:T(8,128)}, f32[4,2,128,128]{3,2,1,0:T(8,128)S(1)}, u32[]{:S(2)}, u32[]{:S(2)}) collective-permute-start(f32[4,2,128,128]{3,2,1,0:T(8,128)} %get-tuple-element.17.sent_o), channel_id=1, source_target_pairs={{1,2},{3,4},{5,6},{2,1},{4,3},{6,5},{9,10},{11,12},{13,14},{10,9},... | collective-permute-start | bytes 1572872 | tf_op jit(solution)/shard_map/ppermute | solution.py:480
  95.1 20.2 %all-to-all-start.3 = ((f32[32,16,128]{2,1,0:T(8,128)}), f32[32,16,128]{2,1,0:T(8,128)S(1)}, u32[]{:S(2)}, u32[]{:S(2)}) async-start(f32[32,16,128]{2,1,0:T(8,128)} %bitcast.16), calls=%async_computation.3 | async-start | bytes 524288 | tf_op jit(solution)/shard_map/all_to_all | solution.py:486

commit v2 on v1

--- a/solution.py
+++ b/solution.py
@@ -126,14 +126,26 @@
     return jnp.concatenate([cot[natural(g, k, r), :] for g in range(4)], axis=0).T
 
 
-def split_kernel(ids, cot, out, send_e, send_o, own, sem):
-    def body(r, _):
-        for k in range(2):
-            own[r, k] = turned(cot, k, r)
-        return 0
-
-    lax.fori_loop(0, ROWS, body, 0)
-    keep = pltpu.make_async_copy(own, out, sem)
+def split_kernel(ids, cot, out, send_e, send_o, held, own, sems):
+    size = TILES * ROWS
+    fetch = [
+        pltpu.make_async_copy(
+            cot.at[size * n:size * (n + 1)], held.at[size * n:size * (n + 1)], sems.at[n])
+        for n in range(8)
+    ]
+    for k in range(2):
+        for g in range(4):
+            fetch[2 * g + k].start()
+    for k in range(2):
+        for g in range(4):
+            fetch[2 * g + k].wait()
+
+        def body(r, _, k=k):
+            own[r, k] = turned(held, k, r)
+            return 0
+
+        lax.fori_loop(0, ROWS, body, 0, unroll=2)
+    keep = pltpu.make_async_copy(own, out, sems.at[0])
     keep.start()
     odd = ids[0] & 1
     for r in range(4):
@@ -207,13 +219,13 @@
 
 def trig_tables(phases, cos_n, sin_n):
     def body(i, _):
-        at = pl.ds(pl.multiple_of(i * 48, 8), 48)
+        at = pl.ds(pl.multiple_of(i * 96, 8), 96)
         s, c = sincos(phases[at, :])
         sin_n[at, :] = s
         cos_n[at, :] = c
         return 0
 
-    lax.fori_loop(0, TILES // 2, body, 0)
+    lax.fori_loop(0, TILES // 4, body, 0)
 
 
 def spread(ref, n):
@@ -225,12 +237,13 @@
     trig_tables(phases, cos_n, sin_n)
 
     def body(i, _):
-        for n in (2 * i, 2 * i + 1):
+        for q in range(4):
+            n = 4 * i + q
             cos_out[n] = spread(cos_n, n)
             sin_out[n] = spread(sin_n, n)
         return 0
 
-    lax.fori_loop(0, LAYERS * ROWS // 2, body, 0)
+    lax.fori_loop(0, LAYERS * ROWS // 4, body, 0)
 
 
 def forward_kernel(ids, angles, ph_e, ph_o, cos_own, sin_own,
@@ -245,13 +258,13 @@
             lo, count = (4 * above, 4) if layer == 1 else (0, 8)
 
             def body(i, _, layer=layer, first=first, lo=lo):
-                for q in range(2):
-                    r = lo + 2 * i + q
+                for q in range(4):
+                    r = lo + 4 * i + q
                     cosr[layer * EXT + first + r] = spread(cos_n, layer * ROWS + r)
                     sinr[layer * EXT + first + r] = spread(sin_n, layer * ROWS + r)
                 return 0
 
-            lax.fori_loop(0, count // 2, body, 0)
+            lax.fori_loop(0, count // 4, body, 0)
     for layer in range(LAYERS):
         def copy(r, _, layer=layer):
             cosr[layer * EXT + HALO + r] = cos_own[layer * ROWS + r]
@@ -340,14 +353,14 @@
 
     def term(layer, adjoint, stored):
         def body(i, _):
-            for r in (2 * i, 2 * i + 1):
+            for r in (4 * i, 4 * i + 1, 4 * i + 2, 4 * i + 3):
                 x = adjoint(r, 1) * stored(r, 0) - adjoint(r, 0) * stored(r, 1)
                 x = x.T
                 x = (x[:TILES] + x[TILES:2 * TILES]) + (x[2 * TILES:3 * TILES] + x[3 * TILES:])
                 terms[pl.ds(layer * ROWS + r, TILES, stride=LAYERS * ROWS), :] = x
             return 0
 
-        lax.fori_loop(0, ROWS // 2, body, 0)
+        lax.fori_loop(0, ROWS // 4, body, 0)
 
     def of(ref, at=0):
         return lambda r, k: ref[at + r, k]
@@ -496,9 +509,9 @@
     dealt = dealt.reshape(2 * PLANE, 2, ROWS, 128)
     got = exchange(dealt, None)
     own, send_e, send_o = call(
-        split_kernel, [sm(), vm()], (field_hbm(8), field(4), field(4)),
-        [scr(8, 2, 128, 128), pltpu.SemaphoreType.DMA], 6, (hbm(), vm(), vm()))(
-            ids, rows_first(cotangent))
+        split_kernel, [sm(), hbm()], (field_hbm(8), field(4), field(4)),
+        [scr(2048, 128), scr(8, 2, 128, 128), pltpu.SemaphoreType.DMA((8,))], 6,
+        (hbm(), vm(), vm()))(ids, in_hbm(rows_first(cotangent)))
     cot_e, cot_o = meet(send_e, send_o, 1)
     whole = call(pick_kernel, [sm(), vm()], shape(PLANE, 2, LAYERS, ROWS, 128), [],
                  2)(ids, got)

time: 117 us -> 115 us (0.983)
  local copies, waits for them, and re-layouts: 1.33 us -> 0.1 us
    unnamed x7 -> x5, local copies, waits for them, and re-layouts: 1.33 us -> 0.1 us
  transfers between devices with their start and end apart: 11 -> 11, of which waited for: 4 -> 4; matrix products, arithmetic and copies ran while one was open for 0% -> 0% of each run, Pallas kernels for 23% -> 22%
where the time goes in v2:
time: 115 us; the launch traced here: 114 us
  Pallas kernels  36.7 us (32%)
  starting transfers between devices  32.9 us (29%)
  waiting for transfers between devices  30.8 us (27%)
  blocking collectives  12.4 us (11%)
    all_to_all x3, waiting for transfers between devices, exchange(): lax.all_to_all(flat, 'illum', 0, 0, axis_index_groups=groups, tiled=True)  25.3 us
    all_to_all x3, starting transfers between devices, exchange(): lax.all_to_all(flat, 'illum', 0, 0, axis_index_groups=groups, tiled=True)  22.1 us
    all_to_all x1, blocking collectives, exchange(): lax.all_to_all(flat, 'illum', 0, 0, axis_index_groups=groups, tiled=True)  12.4 us
    pallas_call x1, Pallas kernels, forward_and_back(): call(forward_kernel, [sm()] * 2 + [vm()] * 4, (shape(LAYERS * EXT, 128, 1...  10.8 us
    ppermute x4, starting transfers between devices, meet(): got_o = lax.ppermute(x_o, 'row', odd)  10 us
    pallas_call x1, Pallas kernels, forward_and_back(): call(back_kernel, [sm()] + [vm()] * 8, shape(TILES * LAYERS * ROWS, 128),...  7.12 us
    ppermute x4, waiting for transfers between devices, meet(): got_o = lax.ppermute(x_o, 'row', odd)  5.55 us
    pallas_call x1, Pallas kernels, forward_and_back(): call(exit_kernel, [sm()] + [hbm()] * 2 + [vm()] * 2, shape(2048, 128), [w...  5.14 us
  transfers between devices with their start and end apart: 11, of which 4 were waited for; matrix products, arithmetic and copies ran while one was open for 0% of the time, Pallas kernels for 22%

profile of v2, /device:TPU:32, one launch (start us, length us, event | category | flops | bytes accessed | tf_op | source)
XLA Modules:
  0.0 114.5 jit_solution(10250351101279817101)
XLA Ops:
  0.6 0.0 copy-start.1
  0.7 0.7 pad_add_fusion.ids
  1.4 3.5 %shard_map.64 = (f32[8,2,128,128]{3,2,1,0:T(8,128)}, f32[4,2,128,128]{3,2,1,0:T(8,128)S(1)}, f32[4,2,128,128]{3,2,1,0:T(8,128)S(1)}) custom-call(s32[5]{0:T(128)S(1)} %pad_add_fusion.ids, f32[2048,128]{1,0:T(8,128)} %bitcast.31), custom_call_target="tpu_custom_call" | custom-call | flops 20000000 | bytes 4194304 | tf_op jit(solution)/shard_map/pallas_call | solution.py:511
  4.9 0.1 collective-permute-start.4
  5.0 3.8 %collective-permute-start.5 = (f32[4,2,128,128]{3,2,1,0:T(8,128)S(1)}, f32[4,2,128,128]{3,2,1,0:T(8,128)S(1)}, u32[]{:S(2)}, u32[]{:S(2)}) collective-permute-start(f32[4,2,128,128]{3,2,1,0:T(8,128)S(1)} %get-tuple-element.25), channel_id=1, source_target_pairs={{1,2},{3,4},{5,6},{2,1},{4,3},{6,5},{9,10},{11,12},{13,14},{10,9},... | collective-permute-start | bytes 1572872 | tf_op jit(solution)/shard_map/ppermute | solution.py:493
  8.8 1.6 %shard_map.59 = f32[2,32,8,128]{3,2,1,0:T(8,128)} custom-call(f32[32,8,128]{2,1,0:T(8,128)} %bitcast.34), custom_call_target="tpu_custom_call" | custom-call | flops 20000000 | bytes 4194304 | tf_op jit(solution)/shard_map/pallas_call | solution.py:506
  10.4 12.3 %all-to-all-start = ((f32[32,16,128]{2,1,0:T(8,128)}), f32[32,16,128]{2,1,0:T(8,128)S(1)}, u32[]{:S(2)}, u32[]{:S(2)}) async-start(f32[32,16,128]{2,1,0:T(8,128)} %bitcast.33), calls=%async_computation | async-start | bytes 524288 | tf_op jit(solution)/shard_map/all_to_all | solution.py:499
  22.7 0.0 collective-permute-done.4.got_e
  22.7 0.0 collective-permute-done.5.got_o
  22.7 4.4 %shard_map.65.w1 = f32[8,2,128,128]{3,2,1,0:T(8,128)} custom-call(s32[5]{0:T(128)S(1)} %pad_add_fusion.ids, f32[8,2,128,128]{3,2,1,0:T(8,128)} %get-tuple-element.23.own, f32[4,2,128,128]{3,2,1,0:T(8,128)S(1)} %collective-permute-done.4.got_e, f32[4,2,128,128]{3,2,1,0:T(8,128)S(1)} %collective-permute-done.5.got_o), custom_call_target="tpu_custom_call" | custom-call | flops 20000000 | bytes 4194304 | tf_op jit(solution)/shard_map/pallas_call | solution.py:519
  27.1 0.0 copy-start
  27.1 0.1 collective-permute-start.6
  27.2 2.4 %collective-permute-start.7 = (f32[8,2,128,128]{3,2,1,0:T(8,128)}, f32[8,2,128,128]{3,2,1,0:T(8,128)S(1)}, u32[]{:S(2)}, u32[]{:S(2)}) collective-permute-start(f32[8,2,128,128]{3,2,1,0:T(8,128)} %shard_map.65.w1), channel_id=1, source_target_pairs={{1,2},{3,4},{5,6},{2,1},{4,3},{6,5},{9,10},{11,12},{13,14},{10,9},... | collective-permute-start | bytes 3145736 | tf_op jit(solution)/shard_map/ppermute | solution.py:493
  29.7 8.1 %all-to-all-done = f32[32,16,128]{2,1,0:T(8,128)S(1)} async-done(((f32[32,16,128]{2,1,0:T(8,128)}), f32[32,16,128]{2,1,0:T(8,128)S(1)}, u32[]{:S(2)}, u32[]{:S(2)}) %all-to-all-start) | async-done | bytes 262176 | tf_op jit(solution)/shard_map/all_to_all | solution.py:499
  37.8 0.6 shard_map.60
  38.4 12.4 %all_to_all.38 = f32[16,48,128]{2,1,0:T(8,128)S(1)} all-to-all(f32[16,48,128]{2,1,0:T(8,128)S(1)} %bitcast.28), channel_id=1, replica_groups={{0,8,16,24,32,40,48,56,64,72,80,88,96,104,112,120},{128,136,144,152,160..., dimensions={0} | all-to-all | bytes 786432 | tf_op jit(solution)/shard_map/all_to_all | solution.py:499
  50.8 0.0 collective-permute-start
  50.8 1.9 %collective-permute-start.1 = (f32[768,128]{1,0:T(8,128)S(1)}, f32[768,128]{1,0:T(8,128)}, u32[]{:S(2)}, u32[]{:S(2)}) collective-permute-start(f32[768,128]{1,0:T(8,128)S(1)} %bitcast.26), channel_id=1, source_target_pairs={{1,2},{3,4},{5,6},{2,1},{4,3},{6,5},{9,10},{11,12},{13,14},{10,9},... | collective-permute-start | bytes 1179656 | tf_op jit(solution)/shard_map/ppermute | solution.py:493
  52.7 0.0 copy-done.1
  52.7 0.1 copy.6.angles
  52.8 1.6 %shard_map.61 = (f32[24,128,128]{2,1,0:T(8,128)S(1)}, f32[24,128,128]{2,1,0:T(8,128)S(1)}) custom-call(f32[768,128]{1,0:T(8,128)S(1)} %bitcast.27), custom_call_target="tpu_custom_call" | custom-call | flops 20000000 | bytes 4194304 | tf_op jit(solution)/shard_map/pallas_call | solution.py:527
  54.4 0.0 collective-permute-done.ph_e
  54.5 5.5 %collective-permute-done.1.ph_o = f32[768,128]{1,0:T(8,128)} collective-permute-done((f32[768,128]{1,0:T(8,128)S(1)}, f32[768,128]{1,0:T(8,128)}, u32[]{:S(2)}, u32[]{:S(2)}) %collective-permute-start.1) | collective-permute-done | bytes 393248 | tf_op jit(solution)/shard_map/ppermute | solution.py:493
  60.0 10.8 %shard_map.62 = (f32[72,128,128]{2,1,0:T(8,128)S(1)}, f32[72,128,128]{2,1,0:T(8,128)S(1)}, f32[8,2,128,128]{3,2,1,0:T(8,128)S(1)}, f32[8,2,128,128]{3,2,1,0:T(8,...) custom-call(s32[5]{0:T(128)S(1)} %pad_add_fusion.ids, ...), custom_call_target="tpu_custom_call" | custom-call | flops 20000000 | bytes 4194304 | tf_op jit(solution)/shard_map/pallas_call | solution.py:530
  70.8 0.0 collective-permute-done.6.w_e
  70.8 0.0 collective-permute-done.7.w_o
  70.8 0.0 copy-done
  70.8 7.1 %shard_map.66 = f32[768,128]{1,0:T(8,128)} custom-call(s32[5]{0:T(128)S(1)} %pad_add_fusion.ids, f32[72,128,128]{2,1,0:T(8,128)S(1)} %get-tuple-element.18.cosr, f32[72,128,128]{2,1,0:T(8,128)S(1)} %get-tuple-element.19.sinr, f32[8,2,128,128]{3,2,1,0:T(8,128)S(1)} %get-tuple-element.20.keep0, f32[8,2,128,128]{3,2,1,0:T(8,128)S(1)} %get-tuple-element.21.keep1, ...), custom_call_target="tpu_custom_call" | custom-call | flops 20000000 | bytes 4194304 | tf_op jit(solution)/shard_map/pallas_call | solution.py:536
  77.9 3.7 %all-to-all-start.2 = ((f32[16,48,128]{2,1,0:T(8,128)}), f32[16,48,128]{2,1,0:T(8,128)S(1)}, u32[]{:S(2)}, u32[]{:S(2)}) async-start(f32[16,48,128]{2,1,0:T(8,128)} %bitcast.14), calls=%async_computation.2 | async-start | bytes 786432 | tf_op jit(solution)/shard_map/all_to_all | solution.py:499
  81.6 0.6 collective-permute-start.2
  82.2 1.9 %collective-permute-start.3 = (f32[4,2,128,128]{3,2,1,0:T(8,128)}, f32[4,2,128,128]{3,2,1,0:T(8,128)S(1)}, u32[]{:S(2)}, u32[]{:S(2)}) collective-permute-start(f32[4,2,128,128]{3,2,1,0:T(8,128)} %get-tuple-element.17.sent_o), channel_id=1, source_target_pairs={{1,2},{3,4},{5,6},{2,1},{4,3},{6,5},{9,10},{11,12},{13,14},{10,9},... | collective-permute-start | bytes 1572872 | tf_op jit(solution)/shard_map/ppermute | solution.py:493
  84.1 8.2 %all-to-all-done.2 = f32[16,48,128]{2,1,0:T(8,128)S(1)} async-done(((f32[16,48,128]{2,1,0:T(8,128)}), f32[16,48,128]{2,1,0:T(8,128)S(1)}, u32[]{:S(2)}, u32[]{:S(2)}) %all-to-all-start.2) | async-done | bytes 393248 | tf_op jit(solution)/shard_map/all_to_all | solution.py:499
  92.3 1.3 %shard_map.67 = f32[32,2,8,128]{3,2,1,0:T(8,128)} custom-call(s32[5]{0:T(128)S(1)} %pad_add_fusion.ids, f32[16,2,3,8,128]{4,3,2,1,0:T(8,128)S(1)} %bitcast.24), custom_call_target="tpu_custom_call" | custom-call | flops 20000000 | bytes 4194304 | tf_op jit(solution)/shard_map/pallas_call | solution.py:542
  93.6 6.1 %all-to-all-start.3 = ((f32[32,16,128]{2,1,0:T(8,128)}), f32[32,16,128]{2,1,0:T(8,128)S(1)}, u32[]{:S(2)}, u32[]{:S(2)}) async-start(f32[32,16,128]{2,1,0:T(8,128)} %bitcast.16), calls=%async_computation.3 | async-start | bytes 524288 | tf_op jit(solution)/shard_map/all_to_all | solution.py:499
  99.7 0.0 collective-permute-done.2.got_e
  99.7 0.0 collective-permute-done.3.got_o
  99.7 5.1 %shard_map.63 = f32[2048,128]{1,0:T(8,128)} custom-call(s32[5]{0:T(128)S(1)} %pad_add_fusion.ids, f32[4,2,128,128]{3,2,1,0:T(8,128)} %get-tuple-element.16.sent_e, f32[4,2,128,128]{3,2,1,0:T(8,128)} %get-tuple-element.17.sent_o, f32[4,2,128,128]{3,2,1,0:T(8,128)S(1)} %collective-permute-done.2.got_e, f32[4,2,128,128]{3,2,1,0:T(8,128)S(1)} %collective-permute-done.3.got_o), custom_call_target="tpu_custom_call" | custom-call | flops 20000000 | bytes 4194304 | tf_op jit(solution)/shard_map/pallas_call | solution.py:545
  104.9 8.9 %all-to-all-done.3 = f32[32,16,128]{2,1,0:T(8,128)S(1)} async-done(((f32[32,16,128]{2,1,0:T(8,128)}), f32[32,16,128]{2,1,0:T(8,128)S(1)}, u32[]{:S(2)}, u32[]{:S(2)}) %all-to-all-start.3) | async-done | bytes 262176 | tf_op jit(solution)/shard_map/all_to_all | solution.py:499
  113.8 0.7 shard_map.68
Async XLA Ops:
  0.6 52.1 %copy-start.1 = (s32[4,2]{0,1:T(2,128)S(1)}, s32[4,2]{0,1:T(2,128)}, u32[]{:S(2)}) copy-start(s32[4,2]{0,1:T(2,128)} %param.4) | copy-start | bytes 100
  4.9 17.8 %collective-permute-start.4 = (f32[4,2,128,128]{3,2,1,0:T(8,128)S(1)}, f32[4,2,128,128]{3,2,1,0:T(8,128)S(1)}, u32[]{:S(2)}, u32[]{:S(2)}) collective-permute-start(f32[4,2,128,128]{3,2,1,0:T(8,128)S(1)} %get-tuple-element.24), channel_id=1, source_target_pairs={{0,1},{1,0},{2,3},{3,2},{4,5},{5,4},{6,7},{7,6},{8,9},{9,8},{10,11... | collective-permute-start | bytes 1572872 | tf_op jit(solution)/shard_map/ppermute | solution.py:494
  5.0 17.7 %collective-permute-start.5 = (f32[4,2,128,128]{3,2,1,0:T(8,128)S(1)}, f32[4,2,128,128]{3,2,1,0:T(8,128)S(1)}, u32[]{:S(2)}, u32[]{:S(2)}) collective-permute-start(f32[4,2,128,128]{3,2,1,0:T(8,128)S(1)} %get-tuple-element.25), channel_id=1, source_target_pairs={{1,2},{3,4},{5,6},{2,1},{4,3},{6,5},{9,10},{11,12},{13,14},{10,9},... | collective-permute-start | bytes 1572872 | tf_op jit(solution)/shard_map/ppermute | solution.py:493
  10.4 27.4 %all-to-all-start = ((f32[32,16,128]{2,1,0:T(8,128)}), f32[32,16,128]{2,1,0:T(8,128)S(1)}, u32[]{:S(2)}, u32[]{:S(2)}) async-start(f32[32,16,128]{2,1,0:T(8,128)} %bitcast.33), calls=%async_computation | async-start | bytes 524288 | tf_op jit(solution)/shard_map/all_to_all | solution.py:499
  27.1 43.7 %copy-start = (f32[8,2,128,128]{3,2,1,0:T(8,128)S(1)}, f32[8,2,128,128]{3,2,1,0:T(8,128)}, u32[]{:S(2)}) copy-start(f32[8,2,128,128]{3,2,1,0:T(8,128)} %shard_map.65.w1) | copy-start | bytes 3145732
  27.1 43.6 %collective-permute-start.6 = (f32[8,2,128,128]{3,2,1,0:T(8,128)}, f32[8,2,128,128]{3,2,1,0:T(8,128)S(1)}, u32[]{:S(2)}, u32[]{:S(2)}) collective-permute-start(f32[8,2,128,128]{3,2,1,0:T(8,128)} %shard_map.65.w1), channel_id=1, source_target_pairs={{0,1},{1,0},{2,3},{3,2},{4,5},{5,4},{6,7},{7,6},{8,9},{9,8},{10,11... | collective-permute-start | bytes 3145736 | tf_op jit(solution)/shard_map/ppermute | solution.py:494
  27.2 43.5 %collective-permute-start.7 = (f32[8,2,128,128]{3,2,1,0:T(8,128)}, f32[8,2,128,128]{3,2,1,0:T(8,128)S(1)}, u32[]{:S(2)}, u32[]{:S(2)}) collective-permute-start(f32[8,2,128,128]{3,2,1,0:T(8,128)} %shard_map.65.w1), channel_id=1, source_target_pairs={{1,2},{3,4},{5,6},{2,1},{4,3},{6,5},{9,10},{11,12},{13,14},{10,9},... | collective-permute-start | bytes 3145736 | tf_op jit(solution)/shard_map/ppermute | solution.py:493
  50.8 3.6 %collective-permute-start = (f32[768,128]{1,0:T(8,128)S(1)}, f32[768,128]{1,0:T(8,128)}, u32[]{:S(2)}, u32[]{:S(2)}) collective-permute-start(f32[768,128]{1,0:T(8,128)S(1)} %bitcast.25), channel_id=1, source_target_pairs={{0,1},{1,0},{2,3},{3,2},{4,5},{5,4},{6,7},{7,6},{8,9},{9,8},{10,11... | collective-permute-start | bytes 1179656 | tf_op jit(solution)/shard_map/ppermute | solution.py:494
  50.8 9.2 %collective-permute-start.1 = (f32[768,128]{1,0:T(8,128)S(1)}, f32[768,128]{1,0:T(8,128)}, u32[]{:S(2)}, u32[]{:S(2)}) collective-permute-start(f32[768,128]{1,0:T(8,128)S(1)} %bitcast.26), channel_id=1, source_target_pairs={{1,2},{3,4},{5,6},{2,1},{4,3},{6,5},{9,10},{11,12},{13,14},{10,9},... | collective-permute-start | bytes 1179656 | tf_op jit(solution)/shard_map/ppermute | solution.py:493
  77.9 14.4 %all-to-all-start.2 = ((f32[16,48,128]{2,1,0:T(8,128)}), f32[16,48,128]{2,1,0:T(8,128)S(1)}, u32[]{:S(2)}, u32[]{:S(2)}) async-start(f32[16,48,128]{2,1,0:T(8,128)} %bitcast.14), calls=%async_computation.2 | async-start | bytes 786432 | tf_op jit(solution)/shard_map/all_to_all | solution.py:499
  81.6 18.1 %collective-permute-start.2 = (f32[4,2,128,128]{3,2,1,0:T(8,128)}, f32[4,2,128,128]{3,2,1,0:T(8,128)S(1)}, u32[]{:S(2)}, u32[]{:S(2)}) collective-permute-start(f32[4,2,128,128]{3,2,1,0:T(8,128)} %get-tuple-element.16.sent_e), channel_id=1, source_target_pairs={{0,1},{1,0},{2,3},{3,2},{4,5},{5,4},{6,7},{7,6},{8,9},{9,8},{10,11... | collective-permute-start | bytes 1572872 | tf_op jit(solution)/shard_map/ppermute | solution.py:494
  82.2 17.5 %collective-permute-start.3 = (f32[4,2,128,128]{3,2,1,0:T(8,128)}, f32[4,2,128,128]{3,2,1,0:T(8,128)S(1)}, u32[]{:S(2)}, u32[]{:S(2)}) collective-permute-start(f32[4,2,128,128]{3,2,1,0:T(8,128)} %get-tuple-element.17.sent_o), channel_id=1, source_target_pairs={{1,2},{3,4},{5,6},{2,1},{4,3},{6,5},{9,10},{11,12},{13,14},{10,9},... | collective-permute-start | bytes 1572872 | tf_op jit(solution)/shard_map/ppermute | solution.py:493
  93.6 20.2 %all-to-all-start.3 = ((f32[32,16,128]{2,1,0:T(8,128)}), f32[32,16,128]{2,1,0:T(8,128)S(1)}, u32[]{:S(2)}, u32[]{:S(2)}) async-start(f32[32,16,128]{2,1,0:T(8,128)} %bitcast.16), calls=%async_computation.3 | async-start | bytes 524288 | tf_op jit(solution)/shard_map/all_to_all | solution.py:499

commit v3 on v2

--- a/solution.py
+++ b/solution.py
@@ -160,7 +160,7 @@
             dst[at + r, k, 8:136, :] = src[r, k]
         return 0
 
-    lax.fori_loop(0, n, body, 0)
+    lax.fori_loop(0, n, body, 0, unroll=2)
 
 
 def adjoint_kernel(ids, own, got_e, got_o, out, own_v, res, u, l1, l2, l3, sem):
@@ -184,7 +184,7 @@
     give.wait()
 
 
-def exit_kernel(ids, sent_e, sent_o, got_e, got_o, out, u, l1, l2, l3, res, held, sems):
+def exit_kernel(ids, sent_e, sent_o, got_e, got_o, out, u, l1, l2, l3, res, held, flat, sems):
     row = ids[0]
     odd = row & 1
     fetch = [
@@ -207,14 +207,24 @@
 
     step(row, u, 16, 4, 4, (l1, l2, l3), rate_scale, write)
 
-    def body(r, _):
-        for k in range(2):
+    size = TILES * ROWS
+    give = [
+        pltpu.make_async_copy(
+            flat.at[size * n:size * (n + 1)], out.at[size * n:size * (n + 1)], sems.at[n])
+        for n in range(8)
+    ]
+    for k in range(2):
+        def body(r, _, k=k):
             x = res[r, k].T
             for g in range(4):
-                out[natural(g, k, r), :] = x[g * TILES:(g + 1) * TILES]
-        return 0
-
-    lax.fori_loop(0, ROWS, body, 0)
+                flat[natural(g, k, r), :] = x[g * TILES:(g + 1) * TILES]
+            return 0
+
+        lax.fori_loop(0, ROWS, body, 0, unroll=2)
+        for g in range(4):
+            give[2 * g + k].start()
+    for c in give:
+        c.wait()
 
 
 def trig_tables(phases, cos_n, sin_n):
@@ -271,7 +281,7 @@
             sinr[layer * EXT + HALO + r] = sin_own[layer * ROWS + r]
             return 0
 
-        lax.fori_loop(0, ROWS, copy, 0)
+        lax.fori_loop(0, ROWS, copy, 0, unroll=2)
 
     lane = lax.broadcasted_iota(jnp.int32, (8, 128), 1)
     sub = lax.broadcasted_iota(jnp.int32, (8, 128), 0)
@@ -336,7 +346,7 @@
             keep1[r, k] = v[HALO + r, k, 8:136, :]
         return 0
 
-    lax.fori_loop(0, ROWS, keep, 0)
+    lax.fori_loop(0, ROWS, keep, 0, unroll=2)
     for c in give:
         c.wait()
 
@@ -374,7 +384,7 @@
                 w[at + r, 1, padded(j), :] = im * c - re * s
             return 0
 
-        lax.fori_loop(0, ROWS, back, 0)
+        lax.fori_loop(0, ROWS, back, 0, unroll=2)
     term(2, of(w1), of(keep2))
     fill_pads(w, EXT)
     clear_outside(row, w, HALO, EXT)
@@ -542,9 +552,11 @@
     send = call(gather_kernel, [sm(), vm()], shape(2 * PLANE, 2, ROWS, 128), [],
                 2)(ids, parts)
     back = exchange(send, None)
-    out = call(exit_kernel, [sm()] + [hbm()] * 2 + [vm()] * 2, shape(2048, 128),
+    out = call(exit_kernel, [sm()] + [hbm()] * 2 + [vm()] * 2,
+               pltpu.HBM((2048, 128), jnp.float32),
                [wide(16)] * 4 + [scr(8, 2, 128, 128), scr(2, 4, 2, 128, 128),
-                                 pltpu.SemaphoreType.DMA((2,))], 13)(
+                                 scr(2048, 128), pltpu.SemaphoreType.DMA((8,))],
+               14, hbm())(
                    ids, in_hbm(last_e), in_hbm(last_o), r_e, r_o)
     grad = call(finish_kernel, [vm()], shape(ROWS, COLS), [], 2)(back)
     out = out.reshape(8, TILES, ROWS, 128).transpose(0, 2, 1, 3)

time: 115 us -> 115 us (level)
  no operation moved by 1% of the time
where the time goes in v3:
time: 115 us; the launch traced here: 114 us
  Pallas kernels  36.5 us (32%)
  starting transfers between devices  32.9 us (29%)
  waiting for transfers between devices  31 us (27%)
  blocking collectives  12.4 us (11%)
    all_to_all x3, waiting for transfers between devices, exchange(): lax.all_to_all(flat, 'illum', 0, 0, axis_index_groups=groups, tiled=True)  25.4 us
    all_to_all x3, starting transfers between devices, exchange(): lax.all_to_all(flat, 'illum', 0, 0, axis_index_groups=groups, tiled=True)  22.1 us
    all_to_all x1, blocking collectives, exchange(): lax.all_to_all(flat, 'illum', 0, 0, axis_index_groups=groups, tiled=True)  12.4 us
    pallas_call x1, Pallas kernels, forward_and_back(): call(forward_kernel, [sm()] * 2 + [vm()] * 4, (shape(LAYERS * EXT, 128, 1...  10.7 us
    ppermute x4, starting transfers between devices, meet(): got_o = lax.ppermute(x_o, 'row', odd)  10 us
    pallas_call x1, Pallas kernels, forward_and_back(): call(back_kernel, [sm()] + [vm()] * 8, shape(TILES * LAYERS * ROWS, 128),...  7.1 us
    ppermute x4, waiting for transfers between devices, meet(): got_o = lax.ppermute(x_o, 'row', odd)  5.55 us
    pallas_call x1, Pallas kernels, forward_and_back(): call(exit_kernel, [sm()] + [hbm()] * 2 + [vm()] * 2, pltpu.HBM((2048, 128...  5 us
  transfers between devices with their start and end apart: 11, of which 4 were waited for; matrix products, arithmetic and copies ran while one was open for 0% of the time, Pallas kernels for 22%

profile of v3, /device:TPU:32, one launch (start us, length us, event | category | flops | bytes accessed | tf_op | source)
XLA Modules:
  0.0 114.4 jit_solution(2905040837691015071)
XLA Ops:
  0.6 0.0 copy-start.1
  0.7 0.7 pad_add_fusion.ids
  1.4 3.5 %shard_map.64 = (f32[8,2,128,128]{3,2,1,0:T(8,128)}, f32[4,2,128,128]{3,2,1,0:T(8,128)S(1)}, f32[4,2,128,128]{3,2,1,0:T(8,128)S(1)}) custom-call(s32[5]{0:T(128)S(1)} %pad_add_fusion.ids, f32[2048,128]{1,0:T(8,128)} %bitcast.31), custom_call_target="tpu_custom_call" | custom-call | flops 20000000 | bytes 4194304 | tf_op jit(solution)/shard_map/pallas_call | solution.py:521
  4.9 0.1 collective-permute-start.4
  5.0 3.8 %collective-permute-start.5 = (f32[4,2,128,128]{3,2,1,0:T(8,128)S(1)}, f32[4,2,128,128]{3,2,1,0:T(8,128)S(1)}, u32[]{:S(2)}, u32[]{:S(2)}) collective-permute-start(f32[4,2,128,128]{3,2,1,0:T(8,128)S(1)} %get-tuple-element.25), channel_id=1, source_target_pairs={{1,2},{3,4},{5,6},{2,1},{4,3},{6,5},{9,10},{11,12},{13,14},{10,9},... | collective-permute-start | bytes 1572872 | tf_op jit(solution)/shard_map/ppermute | solution.py:503
  8.8 1.6 %shard_map.59 = f32[2,32,8,128]{3,2,1,0:T(8,128)} custom-call(f32[32,8,128]{2,1,0:T(8,128)} %bitcast.34), custom_call_target="tpu_custom_call" | custom-call | flops 20000000 | bytes 4194304 | tf_op jit(solution)/shard_map/pallas_call | solution.py:516
  10.4 12.3 %all-to-all-start = ((f32[32,16,128]{2,1,0:T(8,128)}), f32[32,16,128]{2,1,0:T(8,128)S(1)}, u32[]{:S(2)}, u32[]{:S(2)}) async-start(f32[32,16,128]{2,1,0:T(8,128)} %bitcast.33), calls=%async_computation | async-start | bytes 524288 | tf_op jit(solution)/shard_map/all_to_all | solution.py:509
  22.7 0.0 collective-permute-done.4.got_e
  22.7 0.0 collective-permute-done.5.got_o
  22.7 4.4 %shard_map.65.w1 = f32[8,2,128,128]{3,2,1,0:T(8,128)} custom-call(s32[5]{0:T(128)S(1)} %pad_add_fusion.ids, f32[8,2,128,128]{3,2,1,0:T(8,128)} %get-tuple-element.23.own, f32[4,2,128,128]{3,2,1,0:T(8,128)S(1)} %collective-permute-done.4.got_e, f32[4,2,128,128]{3,2,1,0:T(8,128)S(1)} %collective-permute-done.5.got_o), custom_call_target="tpu_custom_call" | custom-call | flops 20000000 | bytes 4194304 | tf_op jit(solution)/shard_map/pallas_call | solution.py:529
  27.1 0.0 copy-start
  27.1 0.1 collective-permute-start.6
  27.2 2.4 %collective-permute-start.7 = (f32[8,2,128,128]{3,2,1,0:T(8,128)}, f32[8,2,128,128]{3,2,1,0:T(8,128)S(1)}, u32[]{:S(2)}, u32[]{:S(2)}) collective-permute-start(f32[8,2,128,128]{3,2,1,0:T(8,128)} %shard_map.65.w1), channel_id=1, source_target_pairs={{1,2},{3,4},{5,6},{2,1},{4,3},{6,5},{9,10},{11,12},{13,14},{10,9},... | collective-permute-start | bytes 3145736 | tf_op jit(solution)/shard_map/ppermute | solution.py:503
  29.7 8.1 %all-to-all-done = f32[32,16,128]{2,1,0:T(8,128)S(1)} async-done(((f32[32,16,128]{2,1,0:T(8,128)}), f32[32,16,128]{2,1,0:T(8,128)S(1)}, u32[]{:S(2)}, u32[]{:S(2)}) %all-to-all-start) | async-done | bytes 262176 | tf_op jit(solution)/shard_map/all_to_all | solution.py:509
  37.8 0.6 shard_map.60
  38.4 12.4 %all_to_all.38 = f32[16,48,128]{2,1,0:T(8,128)S(1)} all-to-all(f32[16,48,128]{2,1,0:T(8,128)S(1)} %bitcast.28), channel_id=1, replica_groups={{0,8,16,24,32,40,48,56,64,72,80,88,96,104,112,120},{128,136,144,152,160..., dimensions={0} | all-to-all | bytes 786432 | tf_op jit(solution)/shard_map/all_to_all | solution.py:509
  50.8 0.0 collective-permute-start
  50.8 1.9 %collective-permute-start.1 = (f32[768,128]{1,0:T(8,128)S(1)}, f32[768,128]{1,0:T(8,128)}, u32[]{:S(2)}, u32[]{:S(2)}) collective-permute-start(f32[768,128]{1,0:T(8,128)S(1)} %bitcast.26), channel_id=1, source_target_pairs={{1,2},{3,4},{5,6},{2,1},{4,3},{6,5},{9,10},{11,12},{13,14},{10,9},... | collective-permute-start | bytes 1179656 | tf_op jit(solution)/shard_map/ppermute | solution.py:503
  52.7 0.0 copy-done.1
  52.7 0.1 copy.6.angles
  52.8 1.6 %shard_map.61 = (f32[24,128,128]{2,1,0:T(8,128)S(1)}, f32[24,128,128]{2,1,0:T(8,128)S(1)}) custom-call(f32[768,128]{1,0:T(8,128)S(1)} %bitcast.27), custom_call_target="tpu_custom_call" | custom-call | flops 20000000 | bytes 4194304 | tf_op jit(solution)/shard_map/pallas_call | solution.py:537
  54.4 0.0 collective-permute-done.ph_e
  54.5 5.5 %collective-permute-done.1.ph_o = f32[768,128]{1,0:T(8,128)} collective-permute-done((f32[768,128]{1,0:T(8,128)S(1)}, f32[768,128]{1,0:T(8,128)}, u32[]{:S(2)}, u32[]{:S(2)}) %collective-permute-start.1) | collective-permute-done | bytes 393248 | tf_op jit(solution)/shard_map/ppermute | solution.py:503
  60.0 10.7 %shard_map.62 = (f32[72,128,128]{2,1,0:T(8,128)S(1)}, f32[72,128,128]{2,1,0:T(8,128)S(1)}, f32[8,2,128,128]{3,2,1,0:T(8,128)S(1)}, f32[8,2,128,128]{3,2,1,0:T(8,...) custom-call(s32[5]{0:T(128)S(1)} %pad_add_fusion.ids, ...), custom_call_target="tpu_custom_call" | custom-call | flops 20000000 | bytes 4194304 | tf_op jit(solution)/shard_map/pallas_call | solution.py:540
  70.7 0.0 collective-permute-done.6.w_e
  70.7 0.0 collective-permute-done.7.w_o
  70.8 0.0 copy-done
  70.8 7.1 %shard_map.66 = f32[768,128]{1,0:T(8,128)} custom-call(s32[5]{0:T(128)S(1)} %pad_add_fusion.ids, f32[72,128,128]{2,1,0:T(8,128)S(1)} %get-tuple-element.18.cosr, f32[72,128,128]{2,1,0:T(8,128)S(1)} %get-tuple-element.19.sinr, f32[8,2,128,128]{3,2,1,0:T(8,128)S(1)} %get-tuple-element.20.keep0, f32[8,2,128,128]{3,2,1,0:T(8,128)S(1)} %get-tuple-element.21.keep1, ...), custom_call_target="tpu_custom_call" | custom-call | flops 20000000 | bytes 4194304 | tf_op jit(solution)/shard_map/pallas_call | solution.py:546
  77.9 3.7 %all-to-all-start.2 = ((f32[16,48,128]{2,1,0:T(8,128)}), f32[16,48,128]{2,1,0:T(8,128)S(1)}, u32[]{:S(2)}, u32[]{:S(2)}) async-start(f32[16,48,128]{2,1,0:T(8,128)} %bitcast.14), calls=%async_computation.2 | async-start | bytes 786432 | tf_op jit(solution)/shard_map/all_to_all | solution.py:509
  81.6 0.6 collective-permute-start.2
  82.2 1.9 %collective-permute-start.3 = (f32[4,2,128,128]{3,2,1,0:T(8,128)}, f32[4,2,128,128]{3,2,1,0:T(8,128)S(1)}, u32[]{:S(2)}, u32[]{:S(2)}) collective-permute-start(f32[4,2,128,128]{3,2,1,0:T(8,128)} %get-tuple-element.17.sent_o), channel_id=1, source_target_pairs={{1,2},{3,4},{5,6},{2,1},{4,3},{6,5},{9,10},{11,12},{13,14},{10,9},... | collective-permute-start | bytes 1572872 | tf_op jit(solution)/shard_map/ppermute | solution.py:503
  84.1 8.2 %all-to-all-done.2 = f32[16,48,128]{2,1,0:T(8,128)S(1)} async-done(((f32[16,48,128]{2,1,0:T(8,128)}), f32[16,48,128]{2,1,0:T(8,128)S(1)}, u32[]{:S(2)}, u32[]{:S(2)}) %all-to-all-start.2) | async-done | bytes 393248 | tf_op jit(solution)/shard_map/all_to_all | solution.py:509
  92.3 1.3 %shard_map.67 = f32[32,2,8,128]{3,2,1,0:T(8,128)} custom-call(s32[5]{0:T(128)S(1)} %pad_add_fusion.ids, f32[16,2,3,8,128]{4,3,2,1,0:T(8,128)S(1)} %bitcast.24), custom_call_target="tpu_custom_call" | custom-call | flops 20000000 | bytes 4194304 | tf_op jit(solution)/shard_map/pallas_call | solution.py:552
  93.5 6.1 %all-to-all-start.3 = ((f32[32,16,128]{2,1,0:T(8,128)}), f32[32,16,128]{2,1,0:T(8,128)S(1)}, u32[]{:S(2)}, u32[]{:S(2)}) async-start(f32[32,16,128]{2,1,0:T(8,128)} %bitcast.16), calls=%async_computation.3 | async-start | bytes 524288 | tf_op jit(solution)/shard_map/all_to_all | solution.py:509
  99.6 0.0 collective-permute-done.2.got_e
  99.7 0.0 collective-permute-done.3.got_o
  99.7 5.0 %shard_map.63 = f32[2048,128]{1,0:T(8,128)} custom-call(s32[5]{0:T(128)S(1)} %pad_add_fusion.ids, f32[4,2,128,128]{3,2,1,0:T(8,128)} %get-tuple-element.16.sent_e, f32[4,2,128,128]{3,2,1,0:T(8,128)} %get-tuple-element.17.sent_o, f32[4,2,128,128]{3,2,1,0:T(8,128)S(1)} %collective-permute-done.2.got_e, f32[4,2,128,128]{3,2,1,0:T(8,128)S(1)} %collective-permute-done.3.got_o), custom_call_target="tpu_custom_call" | custom-call | flops 20000000 | bytes 4194304 | tf_op jit(solution)/shard_map/pallas_call | solution.py:555
  104.7 9.1 %all-to-all-done.3 = f32[32,16,128]{2,1,0:T(8,128)S(1)} async-done(((f32[32,16,128]{2,1,0:T(8,128)}), f32[32,16,128]{2,1,0:T(8,128)S(1)}, u32[]{:S(2)}, u32[]{:S(2)}) %all-to-all-start.3) | async-done | bytes 262176 | tf_op jit(solution)/shard_map/all_to_all | solution.py:509
  113.7 0.7 shard_map.68
Async XLA Ops:
  0.6 52.1 %copy-start.1 = (s32[4,2]{0,1:T(2,128)S(1)}, s32[4,2]{0,1:T(2,128)}, u32[]{:S(2)}) copy-start(s32[4,2]{0,1:T(2,128)} %param.4) | copy-start | bytes 100
  4.9 17.8 %collective-permute-start.4 = (f32[4,2,128,128]{3,2,1,0:T(8,128)S(1)}, f32[4,2,128,128]{3,2,1,0:T(8,128)S(1)}, u32[]{:S(2)}, u32[]{:S(2)}) collective-permute-start(f32[4,2,128,128]{3,2,1,0:T(8,128)S(1)} %get-tuple-element.24), channel_id=1, source_target_pairs={{0,1},{1,0},{2,3},{3,2},{4,5},{5,4},{6,7},{7,6},{8,9},{9,8},{10,11... | collective-permute-start | bytes 1572872 | tf_op jit(solution)/shard_map/ppermute | solution.py:504
  5.0 17.7 %collective-permute-start.5 = (f32[4,2,128,128]{3,2,1,0:T(8,128)S(1)}, f32[4,2,128,128]{3,2,1,0:T(8,128)S(1)}, u32[]{:S(2)}, u32[]{:S(2)}) collective-permute-start(f32[4,2,128,128]{3,2,1,0:T(8,128)S(1)} %get-tuple-element.25), channel_id=1, source_target_pairs={{1,2},{3,4},{5,6},{2,1},{4,3},{6,5},{9,10},{11,12},{13,14},{10,9},... | collective-permute-start | bytes 1572872 | tf_op jit(solution)/shard_map/ppermute | solution.py:503
  10.4 27.3 %all-to-all-start = ((f32[32,16,128]{2,1,0:T(8,128)}), f32[32,16,128]{2,1,0:T(8,128)S(1)}, u32[]{:S(2)}, u32[]{:S(2)}) async-start(f32[32,16,128]{2,1,0:T(8,128)} %bitcast.33), calls=%async_computation | async-start | bytes 524288 | tf_op jit(solution)/shard_map/all_to_all | solution.py:509
  27.1 43.6 %copy-start = (f32[8,2,128,128]{3,2,1,0:T(8,128)S(1)}, f32[8,2,128,128]{3,2,1,0:T(8,128)}, u32[]{:S(2)}) copy-start(f32[8,2,128,128]{3,2,1,0:T(8,128)} %shard_map.65.w1) | copy-start | bytes 3145732
  27.1 43.6 %collective-permute-start.6 = (f32[8,2,128,128]{3,2,1,0:T(8,128)}, f32[8,2,128,128]{3,2,1,0:T(8,128)S(1)}, u32[]{:S(2)}, u32[]{:S(2)}) collective-permute-start(f32[8,2,128,128]{3,2,1,0:T(8,128)} %shard_map.65.w1), channel_id=1, source_target_pairs={{0,1},{1,0},{2,3},{3,2},{4,5},{5,4},{6,7},{7,6},{8,9},{9,8},{10,11... | collective-permute-start | bytes 3145736 | tf_op jit(solution)/shard_map/ppermute | solution.py:504
  27.2 43.5 %collective-permute-start.7 = (f32[8,2,128,128]{3,2,1,0:T(8,128)}, f32[8,2,128,128]{3,2,1,0:T(8,128)S(1)}, u32[]{:S(2)}, u32[]{:S(2)}) collective-permute-start(f32[8,2,128,128]{3,2,1,0:T(8,128)} %shard_map.65.w1), channel_id=1, source_target_pairs={{1,2},{3,4},{5,6},{2,1},{4,3},{6,5},{9,10},{11,12},{13,14},{10,9},... | collective-permute-start | bytes 3145736 | tf_op jit(solution)/shard_map/ppermute | solution.py:503
  50.8 3.6 %collective-permute-start = (f32[768,128]{1,0:T(8,128)S(1)}, f32[768,128]{1,0:T(8,128)}, u32[]{:S(2)}, u32[]{:S(2)}) collective-permute-start(f32[768,128]{1,0:T(8,128)S(1)} %bitcast.25), channel_id=1, source_target_pairs={{0,1},{1,0},{2,3},{3,2},{4,5},{5,4},{6,7},{7,6},{8,9},{9,8},{10,11... | collective-permute-start | bytes 1179656 | tf_op jit(solution)/shard_map/ppermute | solution.py:504
  50.8 9.2 %collective-permute-start.1 = (f32[768,128]{1,0:T(8,128)S(1)}, f32[768,128]{1,0:T(8,128)}, u32[]{:S(2)}, u32[]{:S(2)}) collective-permute-start(f32[768,128]{1,0:T(8,128)S(1)} %bitcast.26), channel_id=1, source_target_pairs={{1,2},{3,4},{5,6},{2,1},{4,3},{6,5},{9,10},{11,12},{13,14},{10,9},... | collective-permute-start | bytes 1179656 | tf_op jit(solution)/shard_map/ppermute | solution.py:503
  77.9 14.4 %all-to-all-start.2 = ((f32[16,48,128]{2,1,0:T(8,128)}), f32[16,48,128]{2,1,0:T(8,128)S(1)}, u32[]{:S(2)}, u32[]{:S(2)}) async-start(f32[16,48,128]{2,1,0:T(8,128)} %bitcast.14), calls=%async_computation.2 | async-start | bytes 786432 | tf_op jit(solution)/shard_map/all_to_all | solution.py:509
  81.6 18.1 %collective-permute-start.2 = (f32[4,2,128,128]{3,2,1,0:T(8,128)}, f32[4,2,128,128]{3,2,1,0:T(8,128)S(1)}, u32[]{:S(2)}, u32[]{:S(2)}) collective-permute-start(f32[4,2,128,128]{3,2,1,0:T(8,128)} %get-tuple-element.16.sent_e), channel_id=1, source_target_pairs={{0,1},{1,0},{2,3},{3,2},{4,5},{5,4},{6,7},{7,6},{8,9},{9,8},{10,11... | collective-permute-start | bytes 1572872 | tf_op jit(solution)/shard_map/ppermute | solution.py:504
  82.2 17.5 %collective-permute-start.3 = (f32[4,2,128,128]{3,2,1,0:T(8,128)}, f32[4,2,128,128]{3,2,1,0:T(8,128)S(1)}, u32[]{:S(2)}, u32[]{:S(2)}) collective-permute-start(f32[4,2,128,128]{3,2,1,0:T(8,128)} %get-tuple-element.17.sent_o), channel_id=1, source_target_pairs={{1,2},{3,4},{5,6},{2,1},{4,3},{6,5},{9,10},{11,12},{13,14},{10,9},... | collective-permute-start | bytes 1572872 | tf_op jit(solution)/shard_map/ppermute | solution.py:503
  93.5 20.2 %all-to-all-start.3 = ((f32[32,16,128]{2,1,0:T(8,128)}), f32[32,16,128]{2,1,0:T(8,128)S(1)}, u32[]{:S(2)}, u32[]{:S(2)}) async-start(f32[32,16,128]{2,1,0:T(8,128)} %bitcast.16), calls=%async_computation.3 | async-start | bytes 524288 | tf_op jit(solution)/shard_map/all_to_all | solution.py:509
